TPU v7x, 256 devices: a whole 4x4x8 slice. The times are simulated.
256 devices in a mesh: lon: 32 (over z, x_lo, core), lat: 8 (over x_hi, y).
Axes of the slice: x: 4 (x_hi: 2, x_lo: 2; x = x_hi * 2 + x_lo), y: 4, z: 8, core: 2. Of those that a mesh axis runs over, the one named last changes fastest.
Arguments:
- potential_heat: float32 [8, 1024, 4096], P(None, 'lat', 'lon'), may hold values from -6 to 6
- saltiness_anomaly: float32 [8, 1024, 4096], P(None, 'lat', 'lon'), may hold values from -6 to 6
- east_current: float32 [8, 1024, 4096], P(None, 'lat', 'lon'), may hold values from -1 to 1
- north_current: float32 [8, 1024, 4096], P(None, 'lat', 'lon'), may hold values from -1 to 1
- water_indicator: int32 [8, 1024, 4096], P(None, 'lat', 'lon'), may hold values from 0 to 1, as said below
- east_west_courant_factor: float32 [1024, 4096], P('lat', 'lon'), may hold values from 0.05 to 0.45
- north_south_courant_factor: float32 [1024, 4096], P('lat', 'lon'), may hold values from 0.05 to 0.45
- interface_diffusion_factor: float32 [7, 1024, 4096], P(None, 'lat', 'lon'), may hold values from 0.05 to 5
- spreading_coefficient: float32 [4, 8], replicated, may hold values from 0.05 to 0.25
- seam_mirror_index: int32 [4096], P('lon'), may hold values from 0 to 4095, as said below
Outputs:
- temperature_next: float32 [8, 1024, 4096], P(None, 'lat', 'lon')
- salinity_next: float32 [8, 1024, 4096], P(None, 'lat', 'lon')
- zonal_next: float32 [8, 1024, 4096], P(None, 'lat', 'lon')
- meridional_next: float32 [8, 1024, 4096], P(None, 'lat', 'lon')
Inputs may be any that keep to these rules, and one draw needn't show every extreme that they name: water_indicator is 0 or 1, and a cell below a land cell is land. seam_mirror_index[i] = (p - i) mod 4096 for one p whose remainder on division by 128 is 127.
All inputs are finite; a program needn't handle non-finite values.
Results may differ from a plain program's by a relative error of at most 0.0003.
Values sent between devices are 32-bit elements; how exact they have to be, the bound alone decides.
No kernel may reach another device: no remote copies, remote signals or barrier semaphores. Data moves between devices by JAX's collectives and lax.ppermute only.
A program may use at most 128 MiB of HBM per device.

v0:
```python
import jax
import jax.numpy as jnp
from jax import lax
from jax.sharding import PartitionSpec as P


def extended_2(cells, sides, width, closed):
    for axis, dim in sides:
        count = lax.axis_size(axis)
        ends = count if closed else count - 1
        head = lax.slice_in_dim(cells, 0, width, axis=dim)
        tail = lax.slice_in_dim(cells, cells.shape[dim] - width, cells.shape[dim], axis=dim)
        cells = jnp.concatenate(
            [
                lax.ppermute(tail, axis, [(i, (i + 1) % count) for i in range(ends)]),
                cells,
                lax.ppermute(head, axis, [((i + 1) % count, i) for i in range(ends)]),
            ],
            axis=dim,
        )
    return cells


def cut(source, first_index, last_index, dimension):
    return lax.slice_in_dim(source, first_index, last_index, axis=dimension)


def ppm_update(extended, courant, opening, dimension):
    length = extended.shape[dimension] - 6
    edge_value = 7.0 / 12.0 * (
        cut(extended, 1, length + 4, dimension) + cut(extended, 2, length + 5, dimension)
    ) - 1.0 / 12.0 * (
        cut(extended, 0, length + 3, dimension) + cut(extended, 3, length + 6, dimension)
    )
    left_edge = cut(edge_value, 0, length + 2, dimension)
    right_edge = cut(edge_value, 1, length + 3, dimension)
    centre = cut(extended, 2, length + 4, dimension)
    slopes = right_edge - left_edge
    curvature = 6.0 * (centre - 0.5 * (left_edge + right_edge))
    courant_size = jnp.abs(courant)
    shape_factor = 1.0 - 2.0 / 3.0 * courant_size
    from_left = cut(right_edge, 0, length + 1, dimension) - 0.5 * courant_size * (
        cut(slopes, 0, length + 1, dimension)
        - shape_factor * cut(curvature, 0, length + 1, dimension)
    )
    from_right = cut(left_edge, 1, length + 2, dimension) + 0.5 * courant_size * (
        cut(slopes, 1, length + 2, dimension)
        + shape_factor * cut(curvature, 1, length + 2, dimension)
    )
    fluxes = courant * opening * jnp.where(courant >= 0.0, from_left, from_right)
    return cut(fluxes, 0, length, dimension) - cut(fluxes, 1, length + 1, dimension)


def face_terms(speed_metric, wet_ext, metric_ext, dimension):
    length = wet_ext.shape[dimension] - 6
    courant = 0.5 * (
        cut(speed_metric, 2, length + 3, dimension) + cut(speed_metric, 3, length + 4, dimension)
    )
    opening = cut(wet_ext, 2, length + 3, dimension) * cut(wet_ext, 3, length + 4, dimension)
    weight = (
        0.5
        * (cut(metric_ext, 2, length + 3, dimension) + cut(metric_ext, 3, length + 4, dimension))
        * opening
    )
    return (courant, opening, weight)


def vertical_solve(target_rhs, coupling):
    layer_total = target_rhs.shape[1]
    zeros_plane = jnp.zeros_like(target_rhs[:, 0])
    factors = []
    reduced = []
    for layer_index in range(layer_total):
        upward = coupling[layer_index - 1] if layer_index > 0 else zeros_plane
        downward = coupling[layer_index] if layer_index < layer_total - 1 else zeros_plane
        divisor = 1.0 + upward + downward
        target = target_rhs[:, layer_index]
        if layer_index > 0:
            divisor = divisor - upward * factors[layer_index - 1]
            target = target + upward * reduced[layer_index - 1]
        factors.append(downward / divisor)
        reduced.append(target / divisor)
    solved_levels = [reduced[layer_total - 1]]
    for layer_index in range(layer_total - 2, -1, -1):
        solved_levels.insert(0, reduced[layer_index] + factors[layer_index] * solved_levels[0])
    return jnp.stack(solved_levels, axis=1)


def fold_rows(block_rows, seam_mirror_index, meridian_total):
    whole_rows = lax.all_gather(block_rows, "lon", axis=2, tiled=True)
    span = block_rows.shape[2]
    tile_number = seam_mirror_index[0] // meridian_total
    piece = lax.dynamic_slice_in_dim(whole_rows, tile_number * span, span, 2)
    return piece[:, :, ::-1]


def shards(
    potential_heat,
    saltiness_anomaly,
    east_current,
    north_current,
    water_indicator,
    east_west_courant_factor,
    north_south_courant_factor,
    interface_diffusion_factor,
    spreading_coefficient,
    seam_mirror_index,
):
    layer_total, parallel_total, meridian_total = potential_heat.shape
    margin = 0
    reach = 3 + margin
    span = meridian_total + 2 * margin
    rise = parallel_total + 2 * margin
    ocean_point_indicator = water_indicator.astype(jnp.float32)
    transported_quantities = jnp.concatenate(
        [
            potential_heat * ocean_point_indicator,
            saltiness_anomaly * ocean_point_indicator,
            east_current * ocean_point_indicator,
            north_current * ocean_point_indicator,
        ],
        axis=0,
    )
    first_stack = jnp.concatenate(
        [
            transported_quantities,
            ocean_point_indicator,
            east_west_courant_factor[None],
            north_south_courant_factor[None],
        ],
        axis=0,
    )
    wide_stack = extended_2(first_stack, (("lon", 2),), reach, True)
    field_x = wide_stack[: 4 * layer_total].reshape(
        4, layer_total, parallel_total, meridian_total + 2 * reach
    )
    wet_x = wide_stack[4 * layer_total : 5 * layer_total]
    metric_x = wide_stack[5 * layer_total : 5 * layer_total + 1]
    speed_x = field_x[2] * metric_x
    courant_x, opening_x, weight_x = face_terms(speed_x, wet_x, metric_x, 2)
    starred = cut(field_x, 3, 3 + span, 3) + ppm_update(field_x, courant_x, opening_x, 3)
    side_planes = cut(wide_stack[3 * layer_total : 5 * layer_total], 3, 3 + span, 2)
    merid_planes = cut(wide_stack[5 * layer_total + 1 :], 3, 3 + span, 2)
    second = jnp.concatenate(
        [starred.reshape(4 * layer_total, parallel_total, span), side_planes, merid_planes], axis=0
    )
    signs_two = jnp.concatenate(
        [
            jnp.ones((2 * layer_total, 1, 1), jnp.float32),
            -jnp.ones((3 * layer_total, 1, 1), jnp.float32),
            jnp.ones((layer_total + 1, 1, 1), jnp.float32),
        ],
        axis=0,
    )
    tall_stack = extended_2(second, (("lat", 1),), reach, False)
    upper_rows = (
        fold_rows(
            second[:, parallel_total - reach :, :][:, ::-1, :], seam_mirror_index, meridian_total
        )
        * signs_two
    )
    northern = lax.axis_index("lat") == lax.axis_size("lat") - 1
    southern = lax.axis_index("lat") == 0
    tall_stack = jnp.concatenate(
        [
            tall_stack[:, : parallel_total + reach],
            jnp.where(northern, upper_rows, tall_stack[:, parallel_total + reach :]),
        ],
        axis=1,
    )
    field_y = tall_stack[: 4 * layer_total].reshape(
        4, layer_total, parallel_total + 2 * reach, span
    )
    merid_speed = tall_stack[4 * layer_total : 5 * layer_total]
    wet_y = tall_stack[5 * layer_total : 6 * layer_total]
    metric_y = tall_stack[6 * layer_total :]
    courant_y, opening_y, weight_y = face_terms(merid_speed * metric_y, wet_y, metric_y, 1)
    advected = cut(field_y, 3, 3 + rise, 2) + ppm_update(field_y, courant_y, opening_y, 2)
    flat_fields = advected.reshape(4 * layer_total, parallel_total, meridian_total)
    near_stack = extended_2(flat_fields, (("lon", 2), ("lat", 1)), 1, True)
    signs_one = signs_two[: 4 * layer_total]
    upper_row = (
        fold_rows(flat_fields[:, parallel_total - 1 :, :], seam_mirror_index, meridian_total)
        * signs_one
    )
    rows_flat = near_stack[:, :, 1:-1]
    lower_row = jnp.where(southern, jnp.zeros_like(rows_flat[:, :1]), rows_flat[:, :1])
    upper_row = jnp.where(northern, upper_row, rows_flat[:, parallel_total + 1 :])
    rows_ext = jnp.concatenate(
        [lower_row, rows_flat[:, 1 : parallel_total + 1], upper_row], axis=1
    ).reshape(4, layer_total, parallel_total + 2, meridian_total)
    cols_ext = near_stack[:, 1:-1, :].reshape(4, layer_total, parallel_total, meridian_total + 2)
    laplacian = (
        weight_x[:, :, 1:] * (cols_ext[..., 2:] - advected)
        - weight_x[:, :, :-1] * (advected - cols_ext[..., :-2])
        + weight_y[:, 1:, :] * (rows_ext[:, :, 2:, :] - advected)
        - weight_y[:, :-1, :] * (advected - rows_ext[:, :, :-2, :])
    )
    diffused = advected + spreading_coefficient[:, :, None, None] * laplacian
    coupling = interface_diffusion_factor * ocean_point_indicator[:-1] * ocean_point_indicator[1:]
    solved = vertical_solve(diffused, coupling) * ocean_point_indicator
    return (solved[0], solved[1], solved[2], solved[3])


def solution(mesh):
    in_specs = (
        P(None, "lat", "lon"),
        P(None, "lat", "lon"),
        P(None, "lat", "lon"),
        P(None, "lat", "lon"),
        P(None, "lat", "lon"),
        P("lat", "lon"),
        P("lat", "lon"),
        P(None, "lat", "lon"),
        P(),
        P("lon"),
    )
    out_specs = (
        P(None, "lat", "lon"),
        P(None, "lat", "lon"),
        P(None, "lat", "lon"),
        P(None, "lat", "lon"),
    )
    return jax.shard_map(shards, mesh=mesh, in_specs=in_specs, out_specs=out_specs, check_vma=False)
```

profile of v0, /device:TPU:1, one launch (start us, length us, event | category | flops | bytes accessed | tf_op | source)
XLA Modules:
  0.0 196.0 jit_solution(4828269922146195840)
XLA Ops:
  8.6 2.0 %copy.86 = f32[8,128,128]{1,2,0:T(8,128)} copy(f32[8,128,128]{2,1,0:T(8,128)} %param.10) | data formatting | bytes 1048576 | tf_op args[0]
  17.3 2.7 %collective-permute-start = (f32[42,128,3]{1,0,2:T(8,128)S(1)}, f32[42,128,3]{1,0,2:T(8,128)S(1)}, u32[]{:S(2)}, u32[]{:S(2)}) collective-permute-start(f32[42,128,3]{1,0,2:T(8,128)S(1)} %copy.92), channel_id=1, source_target_pairs={{0,8},{8,16},{16,24},{24,32},{32,40},{40,48},{48,56},{56,64},{64,7... | collective-permute-start | bytes 193544 | tf_op jit(solution)/shard_map/ppermute | solution.py:15
  22.1 2.0 %copy.99 = f32[8,128,128]{2,1,0:T(8,128)} copy(f32[8,128,128]{1,2,0:T(8,128)} %get-tuple-element.33) | data formatting | bytes 1048576 | tf_op jit(solution)/shard_map/mul | solution.py:120
  31.1 1.8 fusion.38
  33.0 2.0 %copy.98 = f32[32,128,128]{2,1,0:T(8,128)S(1)} copy(f32[32,128,128]{1,2,0:T(8,128)} %bitcast.119) | data formatting | bytes 4194304 | tf_op jit(solution)/shard_map/reshape | solution.py:145
  36.6 2.0 %copy.112 = f32[7,128,128]{1,2,0:T(8,128)} copy(f32[7,128,128]{2,1,0:T(8,128)} %param.17) | data formatting | bytes 917504 | tf_op args[7]
  44.2 1.6 copy.132
  50.5 1.6 copy.117
  56.7 1.6 copy.125
  59.8 1.6 copy.129
  62.1 1.7 slice_bitcast_fusion.10
  64.7 1.6 copy.115
  67.9 1.6 copy.121
  69.4 1.6 copy.124
  72.4 2.5 %collective-permute-start.2 = (f32[49,3,128]{2,1,0:T(4,128)}, f32[49,3,128]{2,1,0:T(4,128)S(1)}, u32[]{:S(2)}, u32[]{:S(2)}) collective-permute-start(f32[49,3,128]{2,1,0:T(4,128)} %copy-done.12), channel_id=1, source_target_pairs={{0,1},{1,2},{2,3},{3,4},{4,5},{5,6},{6,7},{8,9},{9,10},{10,11},{11... | collective-permute-start | bytes 225800 | tf_op jit(solution)/shard_map/ppermute | solution.py:15
  76.5 2.3 %fusion.78 = (f32[8,128,128]{1,2,0:T(8,128)}, f32[8,128,128]{1,2,0:T(8,128)}) fusion(f32[8,128,129]{1,2,0:T(8,128)} %get-tuple-element.24), kind=kLoop, calls=%fused_computation.172 | loop fusion | bytes 2097152 | tf_op jit(solution)/shard_map/slice | solution.py:194
  78.8 2.0 %copy.102 = f32[8,128,128]{2,1,0:T(8,128)} copy(f32[8,128,128]{1,2,0:T(8,128)} %get-tuple-element.50) | data formatting | bytes 1048576 | tf_op jit(solution)/shard_map/slice | solution.py:194
  80.8 2.0 %copy.105 = f32[8,128,128]{2,1,0:T(8,128)} copy(f32[8,128,128]{1,2,0:T(8,128)} %get-tuple-element.51) | data formatting | bytes 1048576 | tf_op jit(solution)/shard_map/slice | solution.py:195
  82.8 27.8 %all-gather.2.cloned.1.call-done = f32[49,3,4096]{2,1,0:T(4,128)} async-done(((f32[49,3,128]{2,1,0:T(4,128)}), f32[49,3,4096]{2,1,0:T(4,128)}) %all-gather.2.cloned.1.call-update) | async-done | bytes 2408464 | tf_op jit(solution)/shard_map/all_gather | solution.py:90
  112.2 1.7 rev.10
  119.6 1.9 fusion.37
  121.5 2.4 %copy.103 = f32[4,8,128,128]{2,1,0,3:T(8,128)S(1)} copy(f32[4,8,128,128]{3,2,1,0:T(8,128)} %fusion.37) | data formatting | bytes 4194304 | tf_op jit(solution)/shard_map/add | solution.py:178
  123.9 2.0 slice.455
  127.6 2.7 %copy.107 = f32[32,1,128]{2,0,1:T(8,128)S(1)} copy(f32[32,1,128]{1,0,2:T(8,128)} %slice.455) | data formatting | bytes 32768 | tf_op jit(solution)/shard_map/slice | solution.py:183
  131.3 33.3 %all_gather.7 = f32[32,1,4096]{2,0,1:T(8,128)S(1)} all-gather(f32[32,1,128]{2,0,1:T(8,128)S(1)} %copy.107), channel_id=1, replica_groups=mesh['lon'=32,'lat'=8] {'lon'}, dimensions={2}, use_global_device_ids=true | all-gather | bytes 540672 | tf_op jit(solution)/shard_map/all_gather | solution.py:90
  164.7 2.1 %fusion.76 = (f32[32,1,130]{1,0,2:T(8,128)S(1)}, f32[32,1,130]{1,0,2:T(8,128)}) fusion(f32[32,128,130]{1,0,2:T(8,128)S(1)} %pad_maximum_fusion.2), kind=kLoop, calls=%fused_computation.170 | loop fusion | bytes 66560 | tf_op jit(solution)/shard_map/slice | solution.py:11
  166.8 3.2 %copy.110 = f32[32,1,130]{2,0,1:T(8,128)S(1)} copy(f32[32,1,130]{1,0,2:T(8,128)} %get-tuple-element.43) | data formatting | bytes 33280 | tf_op jit(solution)/shard_map/slice | solution.py:12
  171.3 1.7 copy.108
  173.0 4.3 %collective-permute-start.6 = (f32[32,1,130]{2,0,1:T(8,128)S(1)}, f32[32,1,130]{2,0,1:T(8,128)S(1)}, u32[]{:S(2)}, u32[]{:S(2)}) collective-permute-start(f32[32,1,130]{2,0,1:T(8,128)S(1)} %copy.108), channel_id=1, source_target_pairs={{1,0},{2,1},{3,2},{4,3},{5,4},{6,5},{7,6},{0,7},{9,8},{10,9},{11,1... | collective-permute-start | bytes 49928 | tf_op jit(solution)/shard_map/ppermute | solution.py:17
  177.3 2.0 %copy.104 = f32[4,8,128,1]{3,2,1,0:T(8,128)} copy(f32[4,8,128,1]{2,1,0,3:T(8,128)S(1)} %bitcast.121) | data formatting | bytes 32768 | tf_op jit(solution)/shard_map/concatenate | solution.py:13
  179.3 2.0 %copy.106 = f32[4,8,128,1]{3,2,1,0:T(8,128)} copy(f32[4,8,128,1]{2,1,0,3:T(8,128)S(1)} %bitcast.122) | data formatting | bytes 32768 | tf_op jit(solution)/shard_map/concatenate | solution.py:13
  182.4 4.2 %fusion.28 = f32[4,8,128,128]{3,2,1,0:T(8,128)S(1)} fusion(f32[4,8,128,128]{3,2,1,0:T(8,128)S(1)} %copy-done.1, f32[4,8,1,128]{3,2,1,0:T(1,128)S(1)} %bitcast.124, f32[4,8,1,128]{3,2,1,0:T(1,128)S(1)} %bitcast.123, f32[4,8,128,1]{3,2,1,0:T(8,128)} %copy.106, f32[4,8,128,1]{3,2,1,0:T(8,128)} %copy.104, f32[8,128,128]{2,1,0:T(8,128)} %get-tuple-element.53, ...), kind=kLoop, calls=%fused_computation.42 | loop fusion | flops 8912896 | bytes 6357120 | tf_op jit(solution)/shard_map/add | solution.py:199
  (168 shorter events, 55.7 us)
Async XLA Ops:
  7.2 4.5 %copy-start.10 = (f32[8,128,128]{2,1,0:T(8,128)S(1)}, f32[8,128,128]{2,1,0:T(8,128)}, u32[]{:S(2)}) copy-start(f32[8,128,128]{2,1,0:T(8,128)} %param.12) | copy-start | bytes 1572868
  7.2 5.4 %copy-start.11 = (f32[8,128,128]{2,1,0:T(8,128)S(1)}, f32[8,128,128]{2,1,0:T(8,128)}, u32[]{:S(2)}) copy-start(f32[8,128,128]{2,1,0:T(8,128)} %param.13) | copy-start | bytes 1572868
  7.2 103.4 %all-gather.2.cloned.1.call-start = ((), (), s32[]{:S(2)}) async-start(), calls=%async_computation | async-start | bytes 3311616 | tf_op jit(solution)/shard_map/all_gather | solution.py:90
  17.3 8.2 %collective-permute-start = (f32[42,128,3]{1,0,2:T(8,128)S(1)}, f32[42,128,3]{1,0,2:T(8,128)S(1)}, u32[]{:S(2)}, u32[]{:S(2)}) collective-permute-start(f32[42,128,3]{1,0,2:T(8,128)S(1)} %copy.92), channel_id=1, source_target_pairs={{0,8},{8,16},{16,24},{24,32},{32,40},{40,48},{48,56},{56,64},{64,7... | collective-permute-start | bytes 193544 | tf_op jit(solution)/shard_map/ppermute | solution.py:15
  20.6 4.9 %collective-permute-start.1 = (f32[42,128,3]{1,0,2:T(8,128)}, f32[42,128,3]{1,0,2:T(8,128)}, u32[]{:S(2)}, u32[]{:S(2)}) collective-permute-start(f32[42,128,3]{1,0,2:T(8,128)} %copy.93), channel_id=1, source_target_pairs={{8,0},{16,8},{24,16},{32,24},{40,32},{48,40},{56,48},{64,56},{72,6... | collective-permute-start | bytes 193544 | tf_op jit(solution)/shard_map/ppermute | solution.py:17
  35.7 6.0 %copy-start.12 = (f32[49,3,128]{2,1,0:T(4,128)}, f32[49,3,128]{2,1,0:T(4,128)S(1)}, u32[]{:S(2)}) copy-start(f32[49,3,128]{2,1,0:T(4,128)S(1)} %get-tuple-element.34) | copy-start | bytes 225796
  72.4 42.5 %collective-permute-start.2 = (f32[49,3,128]{2,1,0:T(4,128)}, f32[49,3,128]{2,1,0:T(4,128)S(1)}, u32[]{:S(2)}, u32[]{:S(2)}) collective-permute-start(f32[49,3,128]{2,1,0:T(4,128)} %copy-done.12), channel_id=1, source_target_pairs={{0,1},{1,2},{2,3},{3,4},{4,5},{5,6},{6,7},{8,9},{9,10},{10,11},{11... | collective-permute-start | bytes 225800 | tf_op jit(solution)/shard_map/ppermute | solution.py:15
  75.0 38.9 %collective-permute-start.3 = (f32[49,3,128]{2,1,0:T(4,128)}, f32[49,3,128]{2,1,0:T(4,128)}, u32[]{:S(2)}, u32[]{:S(2)}) collective-permute-start(f32[49,3,128]{2,1,0:T(4,128)} %get-tuple-element.35), channel_id=1, source_target_pairs={{1,0},{2,1},{3,2},{4,3},{5,4},{6,5},{7,6},{9,8},{10,9},{11,10},{12... | collective-permute-start | bytes 225800 | tf_op jit(solution)/shard_map/ppermute | solution.py:17
  76.5 37.4 %copy-start.34 = (f32[49]{0:T(128)S(1)}, f32[49]{0:T(128)}, u32[]{:S(2)}) copy-start(f32[49]{0:T(128)} %constant.14.clone.1) | copy-start | bytes 592
  123.9 6.4 %copy-start.2 = (f32[8,129,128]{2,1,0:T(8,128)S(1)}, f32[8,129,128]{2,1,0:T(8,128)}, u32[]{:S(2)}) copy-start(f32[8,129,128]{2,1,0:T(8,128)} %get-tuple-element.26) | copy-start | bytes 1585156
  125.8 38.7 %collective-permute-start.4 = (f32[32,128,1]{1,0,2:T(8,128)S(1)}, f32[32,128,1]{1,0,2:T(8,128)S(1)}, u32[]{:S(2)}, u32[]{:S(2)}) collective-permute-start(f32[32,128,1]{1,0,2:T(8,128)S(1)} %get-tuple-element.49), channel_id=1, source_target_pairs={{8,0},{16,8},{24,16},{32,24},{40,32},{48,40},{56,48},{64,56},{72,6... | collective-permute-start | bytes 49160 | tf_op jit(solution)/shard_map/ppermute | solution.py:17
  126.1 38.5 %collective-permute-start.5 = (f32[32,128,1]{1,0,2:T(8,128)S(1)}, f32[32,128,1]{1,0,2:T(8,128)S(1)}, u32[]{:S(2)}, u32[]{:S(2)}) collective-permute-start(f32[32,128,1]{1,0,2:T(8,128)S(1)} %get-tuple-element.48), channel_id=1, source_target_pairs={{0,8},{8,16},{16,24},{24,32},{32,40},{40,48},{48,56},{56,64},{64,7... | collective-permute-start | bytes 49160 | tf_op jit(solution)/shard_map/ppermute | solution.py:15
  170.0 11.3 %collective-permute-start.7 = (f32[32,1,130]{2,0,1:T(8,128)S(1)}, f32[32,1,130]{2,0,1:T(8,128)}, u32[]{:S(2)}, u32[]{:S(2)}) collective-permute-start(f32[32,1,130]{2,0,1:T(8,128)S(1)} %copy.110), channel_id=1, source_target_pairs={{0,1},{1,2},{2,3},{3,4},{4,5},{5,6},{6,7},{7,0},{8,9},{9,10},{10,1... | collective-permute-start | bytes 49928 | tf_op jit(solution)/shard_map/ppermute | solution.py:15
  173.0 9.1 %copy-start.33 = (f32[32]{0:T(128)S(1)}, f32[32]{0:T(128)}, u32[]{:S(2)}) copy-start(f32[32]{0:T(128)} %constant.15.clone.1) | copy-start | bytes 388
  173.0 9.2 %copy-start.1 = (f32[4,8,128,128]{3,2,1,0:T(8,128)S(1)}, f32[4,8,128,128]{3,2,1,0:T(8,128)}, u32[]{:S(2)}) copy-start(f32[4,8,128,128]{3,2,1,0:T(8,128)} %fusion.37) | copy-start | bytes 6291460
  173.0 9.2 %copy-start.4 = (f32[8,128,128]{2,1,0:T(8,128)S(1)}, f32[8,128,128]{2,1,0:T(8,128)}, u32[]{:S(2)}) copy-start(f32[8,128,128]{2,1,0:T(8,128)} %copy.102) | copy-start | bytes 1572868
  173.0 9.2 %copy-start.32 = (f32[4,8]{1,0:T(4,128)S(1)}, f32[4,8]{1,0:T(4,128)}, u32[]{:S(2)}) copy-start(f32[4,8]{1,0:T(4,128)} %param.18) | copy-start | bytes 388
  173.0 9.1 %collective-permute-start.6 = (f32[32,1,130]{2,0,1:T(8,128)S(1)}, f32[32,1,130]{2,0,1:T(8,128)S(1)}, u32[]{:S(2)}, u32[]{:S(2)}) collective-permute-start(f32[32,1,130]{2,0,1:T(8,128)S(1)} %copy.108), channel_id=1, source_target_pairs={{1,0},{2,1},{3,2},{4,3},{5,4},{6,5},{7,6},{0,7},{9,8},{10,9},{11,1... | collective-permute-start | bytes 49928 | tf_op jit(solution)/shard_map/ppermute | solution.py:17
  182.2 4.4 %copy-start.7 = (f32[128,128]{1,0:T(8,128)S(1)}, f32[128,128]{1,0:T(8,128)}, u32[]{:S(2)}) copy-start(f32[128,128]{1,0:T(8,128)} %copy.120) | copy-start | bytes 196612
  182.2 4.4 %copy-start.8 = (f32[128,128]{1,0:T(8,128)S(1)}, f32[128,128]{1,0:T(8,128)}, u32[]{:S(2)}) copy-start(f32[128,128]{1,0:T(8,128)} %copy.132) | copy-start | bytes 196612
  182.2 4.4 %copy-start.13 = (f32[128,128]{1,0:T(8,128)S(1)}, f32[128,128]{1,0:T(8,128)}, u32[]{:S(2)}) copy-start(f32[128,128]{1,0:T(8,128)} %copy.113) | copy-start | bytes 196612
  182.2 4.4 %copy-start.14 = (f32[128,128]{1,0:T(8,128)S(1)}, f32[128,128]{1,0:T(8,128)}, u32[]{:S(2)}) copy-start(f32[128,128]{1,0:T(8,128)} %copy.114) | copy-start | bytes 196612
  182.3 4.4 %copy-start.15 = (f32[128,128]{1,0:T(8,128)S(1)}, f32[128,128]{1,0:T(8,128)}, u32[]{:S(2)}) copy-start(f32[128,128]{1,0:T(8,128)} %copy.116) | copy-start | bytes 196612
  182.3 4.4 %copy-start.16 = (f32[128,128]{1,0:T(8,128)S(1)}, f32[128,128]{1,0:T(8,128)}, u32[]{:S(2)}) copy-start(f32[128,128]{1,0:T(8,128)} %copy.117) | copy-start | bytes 196612
  182.3 4.4 %copy-start.17 = (f32[128,128]{1,0:T(8,128)S(1)}, f32[128,128]{1,0:T(8,128)}, u32[]{:S(2)}) copy-start(f32[128,128]{1,0:T(8,128)} %copy.119) | copy-start | bytes 196612
  182.3 4.4 %copy-start.18 = (f32[128,128]{1,0:T(8,128)S(1)}, f32[128,128]{1,0:T(8,128)}, u32[]{:S(2)}) copy-start(f32[128,128]{1,0:T(8,128)} %copy.122) | copy-start | bytes 196612
  182.3 4.4 %copy-start.19 = (f32[128,128]{1,0:T(8,128)S(1)}, f32[128,128]{1,0:T(8,128)}, u32[]{:S(2)}) copy-start(f32[128,128]{1,0:T(8,128)} %copy.123) | copy-start | bytes 196612
  182.3 4.4 %copy-start.20 = (f32[128,128]{1,0:T(8,128)S(1)}, f32[128,128]{1,0:T(8,128)}, u32[]{:S(2)}) copy-start(f32[128,128]{1,0:T(8,128)} %copy.125) | copy-start | bytes 196612
  182.3 4.4 %copy-start.21 = (f32[128,128]{1,0:T(8,128)S(1)}, f32[128,128]{1,0:T(8,128)}, u32[]{:S(2)}) copy-start(f32[128,128]{1,0:T(8,128)} %copy.128) | copy-start | bytes 196612
  182.3 4.4 %copy-start.22 = (f32[128,128]{1,0:T(8,128)S(1)}, f32[128,128]{1,0:T(8,128)}, u32[]{:S(2)}) copy-start(f32[128,128]{1,0:T(8,128)} %copy.129) | copy-start | bytes 196612
  182.3 4.4 %copy-start.23 = (f32[128,128]{1,0:T(8,128)S(1)}, f32[128,128]{1,0:T(8,128)}, u32[]{:S(2)}) copy-start(f32[128,128]{1,0:T(8,128)} %copy.131) | copy-start | bytes 196612
  182.3 4.4 %copy-start.24 = (f32[128,128]{1,0:T(8,128)S(1)}, f32[128,128]{1,0:T(8,128)}, u32[]{:S(2)}) copy-start(f32[128,128]{1,0:T(8,128)} %copy.115) | copy-start | bytes 196612
  (13 other events, 36.8 us)
Sparse Core Ops, SparseCore 0:
  36.6 74.0 all-gather.1
where the time goes:
time: 198 us; the launch traced here: 196 us
  local copies, waits for them, and re-layouts  78.3 us (40%)
  blocking collectives  33.3 us (17%)
  waiting for transfers between devices  27.8 us (14%)
  other arithmetic  27 us (14%)
  between operations  15 us (8%)
  starting transfers between devices  14.6 us (7%)
    all_gather x1, blocking collectives, fold_rows(): whole_rows = lax.all_gather(block_rows, 'lon', axis=2, tiled=True)  33.3 us
    all_gather x1, waiting for transfers between devices, fold_rows(): whole_rows = lax.all_gather(block_rows, 'lon', axis=2, tiled=True)  27.8 us
    div x14, local copies, waits for them, and re-layouts, vertical_solve(): factors.append(downward / divisor)  18.2 us
    unnamed x84, local copies, waits for them, and re-layouts  9.52 us
    sub x7, local copies, waits for them, and re-layouts, vertical_solve(): divisor = divisor - upward * factors[layer_index - 1]  9.41 us
    ppermute x4, starting transfers between devices, extended_2(): lax.ppermute(tail, axis, [(i, (i + 1) % count) for i in range(ends)])  7.86 us
    ppermute x4, starting transfers between devices, extended_2(): lax.ppermute(head, axis, [((i + 1) % count, i) for i in range(ends)])  6.66 us
    slice x2, local copies, waits for them, and re-layouts, shards(): flat_fields[:, parallel_total - 1:, :]  4.61 us
  transfers between devices with their start and end apart: 9, of which 1 were waited for; matrix products, arithmetic and copies ran while one was open for 31% of the time, Pallas kernels for 0%

commit v1 on v0

v1 whole, which is shorter than its diff:
```python
import functools
import jax
import jax.numpy as jnp
from jax import lax
from jax.experimental import pallas as pl
from jax.experimental.pallas import tpu as pltpu
from jax.sharding import PartitionSpec as P

F32 = jnp.float32
LEVELS = 8
TILE = 8
LANES = 128
VM, DEPTH, METRIC, STRIP, VM_S, DEPTH_S, METRIC_S, PLANES = 32, 40, 41, 42, 44, 45, 46, 47
PAIRS = 24
AD_STRIP, WY, AD_PLANES = 32, 34, 42


def roll(x, shift):
    shift %= LANES
    return x if shift == 0 else pltpu.roll(x, shift, 1)


def turn(x, shift):
    return pltpu.roll(x, shift % TILE, 0)


def iota(dimension):
    return lax.broadcasted_iota(jnp.int32, (TILE, LANES), dimension)


def face_coefs(courant):
    size = jnp.abs(courant)
    rest = 1.0 - size
    edge = courant * rest * (1.0 / 12.0)
    return edge * rest, courant * size * (3.0 - 2.0 * size), edge * size, courant >= 0.0


def edge_sum(before, here, after, beyond):
    return 7.0 * (here + after) - (before + beyond)


def flux_of(coefs, here, after, edge, edge_before, edge_after):
    own, centre, far, positive = coefs
    return own * edge + centre * jnp.where(positive, here, after) - far * jnp.where(positive, edge_before, edge_after)


def pack_kernel(t_ref, s_ref, u_ref, v_ref, w_ref, mx_ref, my_ref, own_ref, ownx_ref, toe_ref, tow_ref):
    fields = (t_ref, s_ref, u_ref, v_ref)
    rows_total = mx_ref.shape[0]
    lane = iota(1)
    low = (lane & 7) < 4
    group = lane >> 3
    zero = jnp.zeros((TILE, LANES), F32)
    for i in range(3):
        ownx_ref[i] = zero

    def body(t, carry):
        rows = pl.ds(pl.multiple_of(t * TILE, TILE), TILE)
        wet = [w_ref[l, rows, :] for l in range(LEVELS)]
        depth = sum(wet[1:], wet[0]).astype(F32)
        packs = []
        for k in range(2):
            pack = zero
            for p in range(16):
                q = jnp.where(wet[p % 8] != 0, fields[2 * k + p // 8][p % 8, rows, :], 0.0)
                pack = jnp.where(group == p, roll(q, 4 + 8 * p), pack)
            packs.append(pack)
            own_ref[k, rows, :] = pack
        toe_ref[rows, :] = jnp.where(low, packs[0], roll(packs[1], 4))
        tow_ref[rows, :] = jnp.where(low, roll(packs[1], -4), packs[0])
        shift = (4 + 8 * t) & (LANES - 1)
        for i, x in enumerate((depth, mx_ref[rows, :], my_ref[rows, :])):
            ownx_ref[i] = jnp.where(group == t, pltpu.roll(x, shift, 1), ownx_ref[i])
        return carry

    lax.fori_loop(0, rows_total // TILE, body, 0)
    depth, metric_x, metric_y = ownx_ref[0], ownx_ref[1], ownx_ref[2]
    first, second = pl.ds(rows_total, TILE), pl.ds(rows_total + TILE, TILE)
    toe_ref[first, :] = jnp.where(low, depth, roll(metric_x, 4))
    toe_ref[second, :] = jnp.where(low, metric_y, 0.0)
    tow_ref[first, :] = jnp.where(low, roll(metric_x, -4), depth)
    tow_ref[second, :] = jnp.where(low, 0.0, metric_y)


def x_tile(t, fields, w_ref, mx_ref, my_ref, own_ref, ownx_ref, fromw_ref, frome_ref, put, put_weight):
    rows_total = mx_ref.shape[0]
    start = t * TILE if isinstance(t, int) else pl.multiple_of(t * TILE, TILE)
    rows = pl.ds(start, TILE)
    lane = iota(1)
    low = (lane & 7) < 4
    group = lane >> 3
    level = (group & 7).astype(F32)
    half = lane < 64
    west, east = fromw_ref[rows, :], frome_ref[rows, :]
    halo = (jnp.where(low, west, east), jnp.where(low, roll(west, -4), roll(east, 4)))
    own = (own_ref[0, rows, :], own_ref[1, rows, :])
    strips = [(jnp.where(low, halo[k], own[k]), jnp.where(low, own[k], halo[k])) for k in range(2)]
    first, second = pl.ds(rows_total, TILE), pl.ds(rows_total + TILE, TILE)
    west, east = fromw_ref[first, :], frome_ref[first, :]
    west_2, east_2 = fromw_ref[second, :], frome_ref[second, :]
    side_halo = (
        jnp.where(low, west, east),
        jnp.where(low, roll(west, -4), roll(east, 4)),
        jnp.where(low, west_2, east_2),
    )

    def spread(x):
        x = jnp.where(group == t, x, 0.0)
        for shift in (8, 16, 32, 64):
            x = x + roll(x, shift)
        return x

    extra = []
    for i in range(3):
        mine = ownx_ref[i]
        extra.append((spread(jnp.where(low, side_halo[i], mine)), spread(jnp.where(low, mine, side_halo[i]))))
    depth_s, mx_s, my_s = extra

    um_s, weight_s, edge_s, flux_s, star_s, vm_s = [], [], [[], []], [[], []], [[], []], []
    for side in range(2):
        mixed = strips[1][side]
        swapped = roll(mixed, 64)
        um = jnp.where(half, mixed, swapped) * mx_s[side]
        vm_s.append(jnp.where(half, swapped, mixed) * my_s[side])
        opening = jnp.minimum(depth_s[side], roll(depth_s[side], -1)) > level
        coefs = face_coefs(jnp.where(opening, 0.5 * (um + roll(um, -1)), 0.0))
        um_s.append(um)
        weight_s.append(jnp.where(opening, 0.5 * (mx_s[side] + roll(mx_s[side], -1)), 0.0))
        for k in range(2):
            q = strips[k][side]
            after = roll(q, -1)
            edge = edge_sum(roll(q, 1), q, after, roll(q, -2))
            flux = flux_of(coefs, q, after, edge, roll(edge, 1), roll(edge, -1))
            edge_s[k].append(edge)
            flux_s[k].append(flux)
            star_s[k].append(q + roll(flux, 1) - flux)
    um_halo = jnp.where(low, um_s[0], um_s[1])
    edge_halo = [jnp.where(low, edge_s[k][0], edge_s[k][1]) for k in range(2)]
    for k in range(2):
        put(STRIP + k, jnp.where(low, star_s[k][0], star_s[k][1]))
    put(VM_S, jnp.where(low, vm_s[0], vm_s[1]))
    put(DEPTH_S, jnp.where(low, depth_s[0], depth_s[1]))
    put(METRIC_S, jnp.where(low, my_s[0], my_s[1]))

    head, tail, heads = lane == 0, lane == LANES - 1, lane < 2
    wet = [w_ref[l, rows, :] for l in range(LEVELS)]
    depth = sum(wet[1:], wet[0]).astype(F32)
    mx, my = mx_ref[rows, :], my_ref[rows, :]
    put(DEPTH, depth)
    put(METRIC, my)
    shallow = jnp.minimum(depth, roll(jnp.where(head, roll(depth_s[1], -4), depth), -1))
    mean_metric = 0.5 * (mx + roll(jnp.where(head, roll(mx_s[1], -4), mx), -1))
    for l in range(LEVELS):
        masked = [jnp.where(wet[l] != 0, field[l, rows, :], 0.0) for field in fields]
        um = masked[2] * mx
        put(VM + l, masked[3] * my)
        opening = shallow > float(l)
        place = 124 - 8 * l
        coefs = face_coefs(
            jnp.where(opening, 0.5 * (um + roll(jnp.where(head, roll(um_halo, place), um), -1)), 0.0)
        )
        if put_weight is not None:
            weight = jnp.where(opening, mean_metric, 0.0)
            put_weight(l, weight)
            put_weight(LEVELS + l, roll(jnp.where(tail, roll(weight_s[0], place), weight), 1))
        for f in range(4):
            q, k = masked[f], f // 2
            place = 124 - 8 * ((f % 2) * 8 + l)
            h = roll(halo[k], place)
            after = roll(jnp.where(head, h, q), -1)
            edge = edge_sum(roll(jnp.where(tail, h, q), 1), q, after, roll(jnp.where(heads, h, q), -2))
            h = roll(edge_halo[k], place)
            flux = flux_of(
                coefs,
                q,
                after,
                edge,
                roll(jnp.where(tail, h, edge), 1),
                roll(jnp.where(head, h, edge), -1),
            )
            h = roll(flux_s[k][0], place)
            put(f * LEVELS + l, q + roll(jnp.where(tail, h, flux), 1) - flux)


def field_planes():
    return [(p, p) for p in range(32)] + [(STRIP, AD_STRIP), (STRIP + 1, AD_STRIP + 1)]


def y_edges(stack, edges, r):
    for p, to in field_planes():
        edges[to, pl.ds(r, TILE), :] = edge_sum(
            stack[p, pl.ds(r - 1, TILE), :],
            stack[p, pl.ds(r, TILE), :],
            stack[p, pl.ds(r + 1, TILE), :],
            stack[p, pl.ds(r + 2, TILE), :],
        )


def y_fluxes(stack, edges, fluxes, advected, r):
    here, after = pl.ds(r, TILE), pl.ds(r + 1, TILE)

    def put(coefs, p, to):
        fluxes[to, here, :] = flux_of(
            coefs,
            stack[p, here, :],
            stack[p, after, :],
            edges[to, here, :],
            edges[to, pl.ds(r - 1, TILE), :],
            edges[to, after, :],
        )

    shallow = jnp.minimum(stack[DEPTH, here, :], stack[DEPTH, after, :])
    mean_metric = 0.5 * (stack[METRIC, here, :] + stack[METRIC, after, :])
    for l in range(LEVELS):
        opening = shallow > float(l)
        coefs = face_coefs(jnp.where(opening, 0.5 * (stack[VM + l, here, :] + stack[VM + l, after, :]), 0.0))
        advected[WY + l, here, :] = jnp.where(opening, mean_metric, 0.0)
        for f in range(4):
            put(coefs, f * LEVELS + l, f * LEVELS + l)
    level = ((iota(1) >> 3) & 7).astype(F32)
    opening = jnp.minimum(stack[DEPTH_S, here, :], stack[DEPTH_S, after, :]) > level
    coefs = face_coefs(jnp.where(opening, 0.5 * (stack[VM_S, here, :] + stack[VM_S, after, :]), 0.0))
    for k in range(2):
        put(coefs, STRIP + k, AD_STRIP + k)


def y_updates(stack, fluxes, advected, r):
    here, before = pl.ds(r, TILE), pl.ds(r - 1, TILE)
    for p, to in field_planes():
        advected[to, here, :] = stack[p, here, :] + fluxes[to, before, :] - fluxes[to, here, :]


def finish(advected, r, depth, weights, coupling, spreading, put):
    lane = iota(1)
    head, tail = lane == 0, lane == LANES - 1
    here, before, after = pl.ds(r, TILE), pl.ds(r - 1, TILE), pl.ds(r + 1, TILE)
    links, factors, inverses = [], [], []
    for l in range(LEVELS):
        divisor = jnp.ones((TILE, LANES), F32)
        if l < LEVELS - 1:
            links.append(jnp.where(depth > float(l + 1), coupling(l), 0.0))
            divisor = divisor + links[l]
        if l > 0:
            divisor = divisor + links[l - 1] - links[l - 1] * factors[l - 1]
        inverses.append(1.0 / divisor)
        if l < LEVELS - 1:
            factors.append(links[l] * inverses[l])
    for f in range(4):
        reduced = []
        for l in range(LEVELS):
            p = f * LEVELS + l
            a = advected[p, here, :]
            h = roll(advected[AD_STRIP + f // 2, here, :], 124 - 8 * ((f % 2) * 8 + l))
            bend = (
                weights(l) * (roll(jnp.where(head, h, a), -1) - a)
                - weights(LEVELS + l) * (a - roll(jnp.where(tail, h, a), 1))
                + advected[WY + l, here, :] * (advected[p, after, :] - a)
                - advected[WY + l, before, :] * (a - advected[p, before, :])
            )
            target = a + spreading[f, l] * bend
            if l > 0:
                target = target + links[l - 1] * reduced[l - 1]
            reduced.append(target * inverses[l])
        solved = reduced[LEVELS - 1]
        put(f * LEVELS + LEVELS - 1, jnp.where(depth > float(LEVELS - 1), solved, 0.0))
        for l in range(LEVELS - 2, -1, -1):
            solved = reduced[l] + factors[l] * solved
            put(f * LEVELS + l, jnp.where(depth > float(l), solved, 0.0))


def swap_lanes(x, stages):
    lane = iota(1)
    for bit in stages:
        x = jnp.where((lane & bit) != 0, roll(x, bit), roll(x, -bit))
    return x


def edge_kernel(
    lat_ref, t_ref, s_ref, u_ref, v_ref, w_ref, mx_ref, my_ref, own_ref, ownx_ref, fromw_ref, frome_ref,
    a_ref, b_ref, edge_ref,
):
    fields = (t_ref, s_ref, u_ref, v_ref)
    rows_total = mx_ref.shape[0]
    for e, t in enumerate((0, rows_total // TILE - 1)):

        def put(p, x, e=e):
            edge_ref[e, p] = x

        x_tile(t, fields, w_ref, mx_ref, my_ref, own_ref, ownx_ref, fromw_ref, frome_ref, put, None)
    sub = iota(0)
    upper = sub < 4
    lat = lat_ref[0]
    even = (lat & 1) == 0
    fold = lat == lat_ref[1] - 1
    negative = set(range(16, 32)) | set(range(VM, VM + LEVELS)) | {STRIP + 1, VM_S}
    for k in range(PAIRS):
        one, two = 2 * k, min(2 * k + 1, PLANES - 1)
        bottom = jnp.where(upper, edge_ref[0, one], turn(edge_ref[0, two], 4))
        top = jnp.where(upper, turn(edge_ref[1, one], 4), edge_ref[1, two])
        mirror = jnp.where((sub & 1) != 0, turn(top, 1), turn(top, -1))
        mirror = jnp.where((sub & 2) != 0, turn(mirror, 2), turn(mirror, -2))
        mirror = swap_lanes(mirror, (1, 2, 4) if one >= STRIP else (1, 2, 4, 8, 16, 32, 64))
        signs = (-1.0 if one in negative else 1.0, -1.0 if two in negative else 1.0)
        if signs[0] == signs[1]:
            mirror = mirror * signs[0]
        else:
            mirror = mirror * jnp.where(upper, signs[0], signs[1])
        a_ref[k] = jnp.where(even, top, bottom)
        b_ref[k] = jnp.where(even, bottom, jnp.where(fold, mirror, top))


def interior_kernel(
    coef_ref, t_ref, s_ref, u_ref, v_ref, w_ref, mx_ref, my_ref, idf_ref, own_ref, ownx_ref, fromw_ref, frome_ref,
    o0, o1, o2, o3, adv_ref, weight_ref,
    stack, edges, fluxes, advected, weights, out, sems,
):
    fields = (t_ref, s_ref, u_ref, v_ref)
    outs = (o0, o1, o2, o3)
    rows_total = mx_ref.shape[0]
    tiles = rows_total // TILE

    def sweep_x(t, carry):
        start = pl.multiple_of(t * TILE, TILE)

        def put(p, x):
            stack[p, pl.ds(start + TILE, TILE), :] = x

        def put_weight(p, x):
            weights[p, pl.ds(start, TILE), :] = x

        x_tile(t, fields, w_ref, mx_ref, my_ref, own_ref, ownx_ref, fromw_ref, frome_ref, put, put_weight)
        return carry

    def sweep_edges(t, carry):
        y_edges(stack, edges, pl.multiple_of(t * TILE + TILE, TILE))
        return carry

    def sweep_y(t, carry):
        r = pl.multiple_of(t * TILE + TILE, TILE)
        y_fluxes(stack, edges, fluxes, advected, r)
        y_updates(stack, fluxes, advected, r)
        return carry

    def copies(t_rows):
        return [
            pltpu.make_async_copy(out.at[pl.ds(f * LEVELS, LEVELS), t_rows, :], outs[f].at[:, t_rows, :], sems.at[f])
            for f in range(4)
        ]

    def sweep_out(t, carry):
        start = pl.multiple_of(t * TILE, TILE)
        rows = pl.ds(start, TILE)
        depth = stack[DEPTH, pl.ds(start + TILE, TILE), :]

        def put(p, x):
            out[p, rows, :] = x

        finish(
            advected, pl.multiple_of(start + TILE, TILE), depth,
            lambda p: weights[p, rows, :], lambda l: idf_ref[l, rows, :], coef_ref, put,
        )
        for copy in copies(rows):
            copy.start()
        return carry

    lax.fori_loop(0, tiles, sweep_x, 0)
    lax.fori_loop(0, tiles, sweep_edges, 0)
    lax.fori_loop(0, tiles, sweep_y, 0)
    lax.fori_loop(1, tiles - 1, sweep_out, 0)
    for e, start in enumerate((0, rows_total - 2 * TILE)):
        adv_ref[:, pl.ds(e * 2 * TILE, 2 * TILE), :] = advected[:, pl.ds(start + TILE, 2 * TILE), :]
    for e, start in enumerate((0, rows_total - TILE)):
        weight_ref[e] = weights[:, pl.ds(start, TILE), :]
    for copy in copies(pl.ds(TILE, rows_total - 2 * TILE)):
        copy.wait()


def border_kernel(
    lat_ref, coef_ref, idf_lo, idf_hi, a_ref, b_ref, edge_ref, adv_ref, weight_ref, i0, i1, i2, i3,
    o0, o1, o2, o3,
    stack, edges, fluxes, advected, out, sems,
):
    outs = (o0, o1, o2, o3)
    rows_total = o0.shape[1]
    even = (lat_ref[0] & 1) == 0
    started = []
    for e in range(2):
        for p in range(PLANES):
            k = p // 2
            if e == 0:
                halo = jnp.where(even, b_ref[k], a_ref[k])
                stack[p, pl.ds(0, TILE), :] = turn(halo, 4) if p % 2 == 0 else halo
            else:
                halo = jnp.where(even, a_ref[k], b_ref[k])
                stack[p, pl.ds(2 * TILE, TILE), :] = halo if p % 2 == 0 else turn(halo, 4)
            stack[p, pl.ds(TILE, TILE), :] = edge_ref[e, p]
        advected[:, pl.ds(TILE if e == 0 else 0, 2 * TILE), :] = adv_ref[:, pl.ds(e * 2 * TILE, 2 * TILE), :]
        y_edges(stack, edges, 5 if e == 0 else 11)
        y_fluxes(stack, edges, fluxes, advected, 6 if e == 0 else 12)
        y_updates(stack, fluxes, advected, 3 if e == 0 else 13)

        def put(p, x, e=e):
            out[e, p] = x

        idf = idf_lo if e == 0 else idf_hi
        finish(
            advected, TILE, stack[DEPTH, pl.ds(TILE, TILE), :],
            lambda p, e=e: weight_ref[e, p], lambda l, idf=idf: idf[l], coef_ref, put,
        )
        rows = pl.ds(0 if e == 0 else rows_total - TILE, TILE)
        for f in range(4):
            copy = pltpu.make_async_copy(
                out.at[e, pl.ds(f * LEVELS, LEVELS)], outs[f].at[:, rows, :], sems.at[e, f]
            )
            copy.start()
            started.append(copy)
    for copy in started:
        copy.wait()


def vmem(n):
    return [pl.BlockSpec(memory_space=pltpu.VMEM)] * n


def anywhere(n):
    return [pl.BlockSpec(memory_space=pl.ANY)] * n


def smem(n):
    return [pl.BlockSpec(memory_space=pltpu.SMEM)] * n


def shape(*dims):
    return jax.ShapeDtypeStruct(dims, F32)


PARAMS = pltpu.CompilerParams(vmem_limit_bytes=40 * 1024 * 1024)


def shards(heat, salt, east, north, water, metric_x, metric_y, diffusion, spreading, mirror):
    rows, cols = metric_x.shape
    lon_count, lat_count = lax.axis_size("lon"), lax.axis_size("lat")
    lon, lat = lax.axis_index("lon"), lax.axis_index("lat")
    lat_info = jnp.stack([lat, jnp.int32(lat_count)]).astype(jnp.int32)
    pivot = (mirror[0] // cols + lon) % lon_count

    base = (heat, salt, east, north, water, metric_x, metric_y)
    own, ownx, to_east, to_west = pl.pallas_call(
        pack_kernel,
        out_shape=(shape(2, rows, LANES), shape(3, TILE, LANES), shape(rows + 16, LANES), shape(rows + 16, LANES)),
        in_specs=vmem(7),
        out_specs=tuple(vmem(4)),
        compiler_params=PARAMS,
    )(*base)
    ring = [(i, (i + 1) % lon_count) for i in range(lon_count)]
    from_west = lax.ppermute(to_east, "lon", ring)
    from_east = lax.ppermute(to_west, "lon", [(j, i) for i, j in ring])
    sides = (own, ownx, from_west, from_east)

    rows_a, rows_b, edge = pl.pallas_call(
        edge_kernel,
        out_shape=(shape(PAIRS, TILE, LANES), shape(PAIRS, TILE, LANES), shape(2, PLANES, TILE, LANES)),
        in_specs=smem(1) + vmem(11),
        out_specs=tuple(vmem(3)),
        compiler_params=PARAMS,
    )(lat_info, *base, *sides)

    index = lambda o, a: o * lat_count + a
    pairs = [(index(o, a), index(o, a ^ 1)) for o in range(lon_count) for a in range(lat_count)]
    got_a = lax.ppermute(rows_a, ("lon", "lat"), pairs)

    def across(k, x):
        fixed = []
        for o in range(lon_count):
            for a in range(1, lat_count - 1):
                fixed.append((index(o, a), index(o, ((a + 1) ^ 1) - 1)))
            fixed.append((index(o, lat_count - 1), index((k - o) % lon_count, lat_count - 1)))
        return lax.ppermute(x, ("lon", "lat"), fixed)

    got_b = lax.switch(pivot, [functools.partial(across, k) for k in range(lon_count)], rows_b)

    stack_rows = rows + 2 * TILE
    results = pl.pallas_call(
        interior_kernel,
        out_shape=(shape(LEVELS, rows, cols),) * 4 + (shape(AD_PLANES, 4 * TILE, LANES), shape(2, 16, TILE, LANES)),
        in_specs=smem(1) + vmem(12),
        out_specs=tuple(anywhere(4) + vmem(2)),
        scratch_shapes=[
            pltpu.VMEM((PLANES, stack_rows, LANES), F32),
            pltpu.VMEM((34, stack_rows, LANES), F32),
            pltpu.VMEM((34, stack_rows, LANES), F32),
            pltpu.VMEM((AD_PLANES, stack_rows, LANES), F32),
            pltpu.VMEM((16, rows, LANES), F32),
            pltpu.VMEM((32, rows, LANES), F32),
            pltpu.SemaphoreType.DMA((4,)),
        ],
        compiler_params=PARAMS,
    )(spreading, *base, diffusion, *sides)
    outs, advected, weights = results[:4], results[4], results[5]

    last = rows // TILE - 1
    return pl.pallas_call(
        border_kernel,
        grid=(1,),
        out_shape=(shape(LEVELS, rows, cols),) * 4,
        in_specs=smem(2)
        + [
            pl.BlockSpec((LEVELS - 1, TILE, cols), lambda i: (0, 0, 0)),
            pl.BlockSpec((LEVELS - 1, TILE, cols), lambda i: (0, last, 0)),
        ]
        + vmem(5)
        + anywhere(4),
        out_specs=tuple(anywhere(4)),
        scratch_shapes=[
            pltpu.VMEM((PLANES, 3 * TILE, LANES), F32),
            pltpu.VMEM((34, 3 * TILE, LANES), F32),
            pltpu.VMEM((34, 3 * TILE, LANES), F32),
            pltpu.VMEM((AD_PLANES, 3 * TILE, LANES), F32),
            pltpu.VMEM((2, 32, TILE, LANES), F32),
            pltpu.SemaphoreType.DMA((2, 4)),
        ],
        input_output_aliases={9 + f: f for f in range(4)},
        compiler_params=PARAMS,
    )(lat_info, spreading, diffusion, diffusion, got_a, got_b, edge, advected, weights, *outs)


def solution(mesh):
    block = P(None, "lat", "lon")
    in_specs = (block,) * 5 + (P("lat", "lon"),) * 2 + (block, P(), P("lon"))
    return jax.shard_map(shards, mesh=mesh, in_specs=in_specs, out_specs=(block,) * 4, check_vma=False)
```

time: 198 us -> 73.8 us (0.37)
  the two profiles are of different devices: /device:TPU:1 before, /device:TPU:103 now
where the time goes in v1:
time: 73.8 us; the launch traced here: 73.3 us
  Pallas kernels  43.8 us (59%)
  waiting for transfers between devices  10.7 us (14%)
  starting transfers between devices  9.34 us (13%)
  local copies, waits for them, and re-layouts  8.34 us (11%)
  between operations  0.94 us (1%)
    pallas_call x1, Pallas kernels, shards(): pl.pallas_call(interior_kernel, out_shape=(shape(LEVELS, rows, cols),) *...  28.3 us
    pallas_call x1, Pallas kernels, shards(): pl.pallas_call(edge_kernel, out_shape=(shape(PAIRS, TILE, LANES), shape(P...  10.6 us
    unnamed x38, local copies, waits for them, and re-layouts  8.34 us
    ppermute x1, waiting for transfers between devices, across(): return lax.ppermute(x, ('lon', 'lat'), fixed)  4.92 us
    ppermute x1, waiting for transfers between devices, shards(): from_east = lax.ppermute(to_west, 'lon', [(j, i) for i, j in ring])  4.48 us
    ppermute x1, starting transfers between devices, across(): return lax.ppermute(x, ('lon', 'lat'), fixed)  4.36 us
    ppermute x1, starting transfers between devices, shards(): from_west = lax.ppermute(to_east, 'lon', ring)  3.68 us
    pallas_call x1, Pallas kernels, shards(): pl.pallas_call(pack_kernel, out_shape=(shape(2, rows, LANES), shape(3, TI...  2.6 us
  transfers between devices with their start and end apart: 4, of which 3 were waited for; matrix products, arithmetic and copies ran while one was open for 0% of the time, Pallas kernels for 39%

profile of v1, /device:TPU:103, one launch (start us, length us, event | category | flops | bytes accessed | tf_op | source)
XLA Modules:
  0.0 73.3 jit_solution(12176447761346680435)
XLA Ops:
  0.6 0.0 copy-start
  0.6 1.0 %copy-done = f32[8,128,128]{2,1,0:T(8,128)S(1)} copy-done((f32[8,128,128]{2,1,0:T(8,128)S(1)}, f32[8,128,128]{2,1,0:T(8,128)}, u32[]{:S(2)}) %copy-start) | copy-done | bytes 524312
  1.7 1.0 %copy-done.2 = f32[8,128,128]{2,1,0:T(8,128)S(1)} copy-done((f32[8,128,128]{2,1,0:T(8,128)S(1)}, f32[8,128,128]{2,1,0:T(8,128)}, u32[]{:S(2)}) %copy-start.2) | copy-done | bytes 524312
  2.7 1.0 %copy-done.4 = f32[8,128,128]{2,1,0:T(8,128)S(1)} copy-done((f32[8,128,128]{2,1,0:T(8,128)S(1)}, f32[8,128,128]{2,1,0:T(8,128)}, u32[]{:S(2)}) %copy-start.4) | copy-done | bytes 524312
  3.8 1.0 %copy-done.6 = f32[8,128,128]{2,1,0:T(8,128)S(1)} copy-done((f32[8,128,128]{2,1,0:T(8,128)S(1)}, f32[8,128,128]{2,1,0:T(8,128)}, u32[]{:S(2)}) %copy-start.6) | copy-done | bytes 524312
  4.8 1.0 %copy-done.8 = s32[8,128,128]{2,1,0:T(8,128)S(1)} copy-done((s32[8,128,128]{2,1,0:T(8,128)S(1)}, s32[8,128,128]{2,1,0:T(8,128)}, u32[]{:S(2)}) %copy-start.8) | copy-done | bytes 524312
  5.8 0.8 %copy-done.11 = f32[128,128]{1,0:T(8,128)S(1)} copy-done((f32[128,128]{1,0:T(8,128)S(1)}, f32[128,128]{1,0:T(8,128)}, u32[]{:S(2)}) %copy-start.11) | copy-done | bytes 65560
  6.7 0.8 %copy-done.13 = f32[128,128]{1,0:T(8,128)S(1)} copy-done((f32[128,128]{1,0:T(8,128)S(1)}, f32[128,128]{1,0:T(8,128)}, u32[]{:S(2)}) %copy-start.13) | copy-done | bytes 65560
  7.5 0.0 copy-start.9
  7.5 0.0 copy-start.12
  7.6 2.6 %shard_map.129 = (f32[2,128,128]{2,1,0:T(8,128)S(1)}, f32[3,8,128]{2,1,0:T(8,128)S(1)}, f32[144,128]{1,0:T(8,128)S(1)}, f32[144,128]{1,0:T(8,128)S(1)}) custom-call(f32[8,128,128]{2,1,0:T(8,128)S(1)} %copy-done, f32[8,128,128]{2,1,0:T(8,128)S(1)} %copy-done.2, f32[8,128,128]{2,1,0:T(8,128)S(1)} %copy-done.4, f32[8,128,128]{2,1,0:T(8,128)S(1)} %copy-done.6, ...), custom_call_target="tpu_custom_call" | custom-call | tf_op jit(solution)/shard_map/pallas_call | solution.py:448
  10.2 3.7 %collective-permute-start.32 = (f32[144,128]{1,0:T(8,128)S(1)}, f32[144,128]{1,0:T(8,128)S(1)}, u32[]{:S(2)}, u32[]{:S(2)}) collective-permute-start(f32[144,128]{1,0:T(8,128)S(1)} %get-tuple-element.84), channel_id=1, source_target_pairs={{0,8},{8,16},{16,24},{24,32},{32,40},{40,48},{48,56},{56,64},{64,7... | collective-permute-start | bytes 221192 | tf_op jit(solution)/shard_map/ppermute | solution.py:456
  13.8 0.0 collective-permute-start.33
  13.8 0.1 pad_add_fusion.lat_ref
  13.9 1.3 %collective-permute-done.32.fromw_ref = f32[144,128]{1,0:T(8,128)S(1)} collective-permute-done((f32[144,128]{1,0:T(8,128)S(1)}, f32[144,128]{1,0:T(8,128)S(1)}, u32[]{:S(2)}, u32[]{:S(2)}) %collective-permute-start.32) | collective-permute-done | bytes 73760 | tf_op jit(solution)/shard_map/ppermute | solution.py:456
  15.3 4.5 %collective-permute-done.33.frome_ref = f32[144,128]{1,0:T(8,128)S(1)} collective-permute-done((f32[144,128]{1,0:T(8,128)S(1)}, f32[144,128]{1,0:T(8,128)S(1)}, u32[]{:S(2)}, u32[]{:S(2)}) %collective-permute-start.33) | collective-permute-done | bytes 73760 | tf_op jit(solution)/shard_map/ppermute | solution.py:457
  19.7 0.0 copy-done.7
  19.8 0.0 copy-done.9
  19.8 0.0 copy-done.12
  19.8 0.0 copy-done.14
  19.8 0.0 copy-start.10
  19.8 10.6 %shard_map.130 = (f32[24,8,128]{2,1,0:T(8,128)}, f32[24,8,128]{2,1,0:T(8,128)}, f32[2,47,8,128]{3,2,1,0:T(8,128)S(1)}) custom-call(s32[2]{0:T(128)S(1)} %pad_add_fusion.lat_ref, f32[8,128,128]{2,1,0:T(8,128)S(1)} %copy-done.1, f32[8,128,128]{2,1,0:T(8,128)S(1)} %copy-done.3, f32[8,128,128]{2,1,0:T(8,128)S(1)} %copy-done.5, f32[8,128,128]{2,1,0:T(8,128)S(1)} %copy-done.7, ...), custom_call_target="tpu_custom_call" | custom-call | tf_op jit(solution)/shard_map/pallas_call | solution.py:460
  30.3 0.8 %copy-done.15 = f32[2,47,8,128]{3,2,1,0:T(8,128)} copy-done((f32[2,47,8,128]{3,2,1,0:T(8,128)}, f32[2,47,8,128]{3,2,1,0:T(8,128)S(1)}, u32[]{:S(2)}) %copy-start.15) | copy-done | bytes 385048
  31.1 1.3 %collective-permute-start.34 = (f32[24,8,128]{2,1,0:T(8,128)}, f32[24,8,128]{2,1,0:T(8,128)}, u32[]{:S(2)}, u32[]{:S(2)}) collective-permute-start(f32[24,8,128]{2,1,0:T(8,128)} %get-tuple-element.86), channel_id=1, source_target_pairs={{0,1},{1,0},{2,3},{3,2},{4,5},{5,4},{6,7},{7,6},{8,9},{9,8},{10,11... | collective-permute-start | bytes 294920 | tf_op jit(solution)/shard_map/ppermute | solution.py:470
  32.4 0.7 copy-done.18
  33.2 0.0 copy-start.17
  33.3 9.3 %conditional.1 = (f32[24,8,128]{2,1,0:T(8,128)}) conditional(s32[]{:T(128)} %clamp.3, f32[24,8,128]{2,1,0:T(8,128)} %get-tuple-element.87, f32[24,8,128]{2,1,0:T(8,128)} %get-tuple-element.87, f32[24,8,128]{2,1,0:T(8,128)} %get-tuple-element.87, f32[24,8,128]{2,1,0:T(8,128)} %get-tuple-element.87, ...), branch_computations={%region_0.1_spmd, %region_1.2_spmd, %region_2.3_spmd, %region_3.4_... | conditional | bytes 393264 | solution.py:480
  33.3 4.4 %collective-permute-start.15 = (f32[24,8,128]{2,1,0:T(8,128)}, f32[24,8,128]{2,1,0:T(8,128)}, u32[]{:S(2)}, u32[]{:S(2)}) collective-permute-start(f32[24,8,128]{2,1,0:T(8,128)} %param.15), channel_id=1, source_target_pairs={{1,2},{2,1},{3,4},{4,3},{5,6},{6,5},{7,127},{9,10},{10,9},{11,12},... | collective-permute-start | bytes 294920 | tf_op jit(solution)/shard_map/cond/branch_15_fun/ppermute | solution.py:478
  37.7 4.9 %collective-permute-done.15 = f32[24,8,128]{2,1,0:T(8,128)} collective-permute-done((f32[24,8,128]{2,1,0:T(8,128)}, f32[24,8,128]{2,1,0:T(8,128)}, u32[]{:S(2)}, u32[]{:S(2)}) %collective-permute-start.15) | collective-permute-done | bytes 98336 | tf_op jit(solution)/shard_map/cond/branch_15_fun/ppermute | solution.py:478
  42.6 28.3 %shard_map.131 = (f32[8,128,128]{2,1,0:T(8,128)}, f32[8,128,128]{2,1,0:T(8,128)}, f32[8,128,128]{2,1,0:T(8,128)}, f32[8,128,128]{2,1,0:T(8,128)}, f32[42,32,128]...) custom-call(f32[4,8]{1,0:T(4,128)S(1)} %copy-done.17, f32[8,128,128]{2,1,0:T(8,128)S(1)} %copy-done.1, ...), custom_call_target="tpu_custom_call" | custom-call | tf_op jit(solution)/shard_map/pallas_call | solution.py:483
  70.9 0.0 collective-permute-done.34.a_ref
  71.0 2.3 %shard_map.132 = (f32[8,128,128]{2,1,0:T(8,128)}, f32[8,128,128]{2,1,0:T(8,128)}, f32[8,128,128]{2,1,0:T(8,128)}, f32[8,128,128]{2,1,0:T(8,128)}) custom-call(s32[2]{0:T(128)S(1)} %pad_add_fusion.lat_ref, f32[4,8]{1,0:T(4,128)S(1)} %copy-done.17, ...), custom_call_target="tpu_custom_call", output_to_operand_aliasing={{0}: (9, {}), {1}: (10, {}), {2}: (11, {}), {3}: (12, {})} | custom-call | tf_op jit(solution)/shard_map/pallas_call | solution.py:502
  (20 shorter events, 0.0 us)
Async XLA Ops:
  0.6 1.0 %copy-start = (f32[8,128,128]{2,1,0:T(8,128)S(1)}, f32[8,128,128]{2,1,0:T(8,128)}, u32[]{:S(2)}) copy-start(f32[8,128,128]{2,1,0:T(8,128)} %t_ref.5) | copy-start | bytes 1572868
  1.7 1.0 %copy-start.2 = (f32[8,128,128]{2,1,0:T(8,128)S(1)}, f32[8,128,128]{2,1,0:T(8,128)}, u32[]{:S(2)}) copy-start(f32[8,128,128]{2,1,0:T(8,128)} %s_ref.5) | copy-start | bytes 1572868
  2.7 1.0 %copy-start.4 = (f32[8,128,128]{2,1,0:T(8,128)S(1)}, f32[8,128,128]{2,1,0:T(8,128)}, u32[]{:S(2)}) copy-start(f32[8,128,128]{2,1,0:T(8,128)} %u_ref.5) | copy-start | bytes 1572868
  3.8 1.0 %copy-start.6 = (f32[8,128,128]{2,1,0:T(8,128)S(1)}, f32[8,128,128]{2,1,0:T(8,128)}, u32[]{:S(2)}) copy-start(f32[8,128,128]{2,1,0:T(8,128)} %v_ref.5) | copy-start | bytes 1572868
  4.8 1.0 %copy-start.8 = (s32[8,128,128]{2,1,0:T(8,128)S(1)}, s32[8,128,128]{2,1,0:T(8,128)}, u32[]{:S(2)}) copy-start(s32[8,128,128]{2,1,0:T(8,128)} %w_ref.5) | copy-start | bytes 1572868
  5.8 0.8 %copy-start.11 = (f32[128,128]{1,0:T(8,128)S(1)}, f32[128,128]{1,0:T(8,128)}, u32[]{:S(2)}) copy-start(f32[128,128]{1,0:T(8,128)} %mx_ref.5) | copy-start | bytes 196612
  6.7 0.8 %copy-start.13 = (f32[128,128]{1,0:T(8,128)S(1)}, f32[128,128]{1,0:T(8,128)}, u32[]{:S(2)}) copy-start(f32[128,128]{1,0:T(8,128)} %my_ref.5) | copy-start | bytes 196612
  7.5 12.2 %copy-start.1 = (f32[8,128,128]{2,1,0:T(8,128)S(1)}, f32[8,128,128]{2,1,0:T(8,128)}, u32[]{:S(2)}) copy-start(f32[8,128,128]{2,1,0:T(8,128)} %t_ref.5) | copy-start | bytes 1572868
  7.5 12.2 %copy-start.3 = (f32[8,128,128]{2,1,0:T(8,128)S(1)}, f32[8,128,128]{2,1,0:T(8,128)}, u32[]{:S(2)}) copy-start(f32[8,128,128]{2,1,0:T(8,128)} %s_ref.5) | copy-start | bytes 1572868
  7.5 12.2 %copy-start.5 = (f32[8,128,128]{2,1,0:T(8,128)S(1)}, f32[8,128,128]{2,1,0:T(8,128)}, u32[]{:S(2)}) copy-start(f32[8,128,128]{2,1,0:T(8,128)} %u_ref.5) | copy-start | bytes 1572868
  7.5 12.2 %copy-start.7 = (f32[8,128,128]{2,1,0:T(8,128)S(1)}, f32[8,128,128]{2,1,0:T(8,128)}, u32[]{:S(2)}) copy-start(f32[8,128,128]{2,1,0:T(8,128)} %v_ref.5) | copy-start | bytes 1572868
  7.5 12.2 %copy-start.9 = (s32[8,128,128]{2,1,0:T(8,128)S(1)}, s32[8,128,128]{2,1,0:T(8,128)}, u32[]{:S(2)}) copy-start(s32[8,128,128]{2,1,0:T(8,128)} %w_ref.5) | copy-start | bytes 1572868
  7.5 12.2 %copy-start.12 = (f32[128,128]{1,0:T(8,128)S(1)}, f32[128,128]{1,0:T(8,128)}, u32[]{:S(2)}) copy-start(f32[128,128]{1,0:T(8,128)} %mx_ref.5) | copy-start | bytes 196612
  7.6 12.2 %copy-start.14 = (f32[128,128]{1,0:T(8,128)S(1)}, f32[128,128]{1,0:T(8,128)}, u32[]{:S(2)}) copy-start(f32[128,128]{1,0:T(8,128)} %my_ref.5) | copy-start | bytes 196612
  10.2 5.1 %collective-permute-start.32 = (f32[144,128]{1,0:T(8,128)S(1)}, f32[144,128]{1,0:T(8,128)S(1)}, u32[]{:S(2)}, u32[]{:S(2)}) collective-permute-start(f32[144,128]{1,0:T(8,128)S(1)} %get-tuple-element.84), channel_id=1, source_target_pairs={{0,8},{8,16},{16,24},{24,32},{32,40},{40,48},{48,56},{56,64},{64,7... | collective-permute-start | bytes 221192 | tf_op jit(solution)/shard_map/ppermute | solution.py:456
  13.8 5.9 %collective-permute-start.33 = (f32[144,128]{1,0:T(8,128)S(1)}, f32[144,128]{1,0:T(8,128)S(1)}, u32[]{:S(2)}, u32[]{:S(2)}) collective-permute-start(f32[144,128]{1,0:T(8,128)S(1)} %get-tuple-element.85), channel_id=1, source_target_pairs={{8,0},{16,8},{24,16},{32,24},{40,32},{48,40},{56,48},{64,56},{72,6... | collective-permute-start | bytes 221192 | tf_op jit(solution)/shard_map/ppermute | solution.py:457
  19.8 22.8 %copy-start.10 = (f32[7,128,128]{2,1,0:T(8,128)S(1)}, f32[7,128,128]{2,1,0:T(8,128)}, u32[]{:S(2)}) copy-start(f32[7,128,128]{2,1,0:T(8,128)} %idf_hi.1) | copy-start | bytes 1376260
  30.3 0.8 %copy-start.15 = (f32[2,47,8,128]{3,2,1,0:T(8,128)}, f32[2,47,8,128]{3,2,1,0:T(8,128)S(1)}, u32[]{:S(2)}) copy-start(f32[2,47,8,128]{3,2,1,0:T(8,128)S(1)} %get-tuple-element.88.edge_ref) | copy-start | bytes 1155076
  31.1 39.8 %collective-permute-start.34 = (f32[24,8,128]{2,1,0:T(8,128)}, f32[24,8,128]{2,1,0:T(8,128)}, u32[]{:S(2)}, u32[]{:S(2)}) collective-permute-start(f32[24,8,128]{2,1,0:T(8,128)} %get-tuple-element.86), channel_id=1, source_target_pairs={{0,1},{1,0},{2,3},{3,2},{4,5},{5,4},{6,7},{7,6},{8,9},{9,8},{10,11... | collective-permute-start | bytes 294920 | tf_op jit(solution)/shard_map/ppermute | solution.py:470
  32.4 0.7 copy-start.18
  33.2 9.3 %copy-start.17 = (f32[4,8]{1,0:T(4,128)S(1)}, f32[4,8]{1,0:T(4,128)}, u32[]{:S(2)}) copy-start(f32[4,8]{1,0:T(4,128)} %coef_ref.3) | copy-start | bytes 388
  33.3 9.3 %collective-permute-start.15 = (f32[24,8,128]{2,1,0:T(8,128)}, f32[24,8,128]{2,1,0:T(8,128)}, u32[]{:S(2)}, u32[]{:S(2)}) collective-permute-start(f32[24,8,128]{2,1,0:T(8,128)} %param.15), channel_id=1, source_target_pairs={{1,2},{2,1},{3,4},{4,3},{5,6},{6,5},{7,127},{9,10},{10,9},{11,12},... | collective-permute-start | bytes 294920 | tf_op jit(solution)/shard_map/cond/branch_15_fun/ppermute | solution.py:478
  42.6 28.4 %copy-start.16 = (f32[2,47,8,128]{3,2,1,0:T(8,128)S(1)}, f32[2,47,8,128]{3,2,1,0:T(8,128)}, u32[]{:S(2)}) copy-start(f32[2,47,8,128]{3,2,1,0:T(8,128)} %copy-done.15) | copy-start | bytes 1155076

commit v2 on v1

--- a/solution.py
+++ b/solution.py
@@ -46,16 +46,22 @@
 
 def pack_kernel(t_ref, s_ref, u_ref, v_ref, w_ref, mx_ref, my_ref, own_ref, ownx_ref, toe_ref, tow_ref):
     fields = (t_ref, s_ref, u_ref, v_ref)
-    rows_total = mx_ref.shape[0]
+    step, tiles = pl.program_id(0), mx_ref.shape[0] // TILE
+    rows_total = toe_ref.shape[0] - 2 * TILE
     lane = iota(1)
     low = (lane & 7) < 4
     group = lane >> 3
     zero = jnp.zeros((TILE, LANES), F32)
-    for i in range(3):
-        ownx_ref[i] = zero
+
+    @pl.when(step == 0)
+    def _():
+        for i in range(3):
+            ownx_ref[i] = zero
 
     def body(t, carry):
         rows = pl.ds(pl.multiple_of(t * TILE, TILE), TILE)
+        tile = t + step * tiles
+        whole = pl.ds(pl.multiple_of(tile * TILE, TILE), TILE)
         wet = [w_ref[l, rows, :] for l in range(LEVELS)]
         depth = sum(wet[1:], wet[0]).astype(F32)
         packs = []
@@ -66,25 +72,28 @@
                 pack = jnp.where(group == p, roll(q, 4 + 8 * p), pack)
             packs.append(pack)
             own_ref[k, rows, :] = pack
-        toe_ref[rows, :] = jnp.where(low, packs[0], roll(packs[1], 4))
-        tow_ref[rows, :] = jnp.where(low, roll(packs[1], -4), packs[0])
-        shift = (4 + 8 * t) & (LANES - 1)
+        toe_ref[whole, :] = jnp.where(low, packs[0], roll(packs[1], 4))
+        tow_ref[whole, :] = jnp.where(low, roll(packs[1], -4), packs[0])
+        shift = (4 + 8 * tile) & (LANES - 1)
         for i, x in enumerate((depth, mx_ref[rows, :], my_ref[rows, :])):
-            ownx_ref[i] = jnp.where(group == t, pltpu.roll(x, shift, 1), ownx_ref[i])
-        return carry
-
-    lax.fori_loop(0, rows_total // TILE, body, 0)
-    depth, metric_x, metric_y = ownx_ref[0], ownx_ref[1], ownx_ref[2]
-    first, second = pl.ds(rows_total, TILE), pl.ds(rows_total + TILE, TILE)
-    toe_ref[first, :] = jnp.where(low, depth, roll(metric_x, 4))
-    toe_ref[second, :] = jnp.where(low, metric_y, 0.0)
-    tow_ref[first, :] = jnp.where(low, roll(metric_x, -4), depth)
-    tow_ref[second, :] = jnp.where(low, 0.0, metric_y)
+            ownx_ref[i] = jnp.where(group == tile, pltpu.roll(x, shift, 1), ownx_ref[i])
+        return carry
+
+    lax.fori_loop(0, tiles, body, 0)
+
+    @pl.when(step == pl.num_programs(0) - 1)
+    def _():
+        depth, metric_x, metric_y = ownx_ref[0], ownx_ref[1], ownx_ref[2]
+        first, second = pl.ds(rows_total, TILE), pl.ds(rows_total + TILE, TILE)
+        toe_ref[first, :] = jnp.where(low, depth, roll(metric_x, 4))
+        toe_ref[second, :] = jnp.where(low, metric_y, 0.0)
+        tow_ref[first, :] = jnp.where(low, roll(metric_x, -4), depth)
+        tow_ref[second, :] = jnp.where(low, 0.0, metric_y)
 
 
 def x_tile(t, fields, w_ref, mx_ref, my_ref, own_ref, ownx_ref, fromw_ref, frome_ref, put, put_weight):
     rows_total = mx_ref.shape[0]
-    start = t * TILE if isinstance(t, int) else pl.multiple_of(t * TILE, TILE)
+    start = pl.multiple_of(t * TILE, TILE)
     rows = pl.ds(start, TILE)
     lane = iota(1)
     low = (lane & 7) < 4
@@ -268,45 +277,50 @@
             put(f * LEVELS + l, jnp.where(depth > float(l), solved, 0.0))
 
 
-def swap_lanes(x, stages):
-    lane = iota(1)
-    for bit in stages:
-        x = jnp.where((lane & bit) != 0, roll(x, bit), roll(x, -bit))
-    return x
-
-
 def edge_kernel(
     lat_ref, t_ref, s_ref, u_ref, v_ref, w_ref, mx_ref, my_ref, own_ref, ownx_ref, fromw_ref, frome_ref,
     a_ref, b_ref, edge_ref,
 ):
     fields = (t_ref, s_ref, u_ref, v_ref)
-    rows_total = mx_ref.shape[0]
-    for e, t in enumerate((0, rows_total // TILE - 1)):
-
-        def put(p, x, e=e):
+    tiles = mx_ref.shape[0] // TILE
+
+    def sweep(e, carry):
+        def put(p, x):
             edge_ref[e, p] = x
 
-        x_tile(t, fields, w_ref, mx_ref, my_ref, own_ref, ownx_ref, fromw_ref, frome_ref, put, None)
-    sub = iota(0)
+        x_tile(e * (tiles - 1), fields, w_ref, mx_ref, my_ref, own_ref, ownx_ref, fromw_ref, frome_ref, put, None)
+        return carry
+
+    lax.fori_loop(0, 2, sweep, 0)
+    lane, sub = iota(1), iota(0)
     upper = sub < 4
     lat = lat_ref[0]
     even = (lat & 1) == 0
     fold = lat == lat_ref[1] - 1
-    negative = set(range(16, 32)) | set(range(VM, VM + LEVELS)) | {STRIP + 1, VM_S}
-    for k in range(PAIRS):
-        one, two = 2 * k, min(2 * k + 1, PLANES - 1)
+
+    def send(k, lanes, first_sign, second_sign):
+        one, two = 2 * k, 2 * k + 1
         bottom = jnp.where(upper, edge_ref[0, one], turn(edge_ref[0, two], 4))
         top = jnp.where(upper, turn(edge_ref[1, one], 4), edge_ref[1, two])
         mirror = jnp.where((sub & 1) != 0, turn(top, 1), turn(top, -1))
         mirror = jnp.where((sub & 2) != 0, turn(mirror, 2), turn(mirror, -2))
-        mirror = swap_lanes(mirror, (1, 2, 4) if one >= STRIP else (1, 2, 4, 8, 16, 32, 64))
-        signs = (-1.0 if one in negative else 1.0, -1.0 if two in negative else 1.0)
-        if signs[0] == signs[1]:
-            mirror = mirror * signs[0]
-        else:
-            mirror = mirror * jnp.where(upper, signs[0], signs[1])
+        mirror = jnp.take_along_axis(mirror, lanes, axis=1) * jnp.where(upper, first_sign, second_sign)
         a_ref[k] = jnp.where(even, top, bottom)
         b_ref[k] = jnp.where(even, bottom, jnp.where(fold, mirror, top))
+
+    def send_plain(i, carry):
+        for k in range(3):
+            pair = i * 3 + k
+            sign = jnp.where((pair >= 8) & (pair < 20), -1.0, 1.0)
+            send(pair, LANES - 1 - lane, sign, sign)
+        return carry
+
+    lax.fori_loop(0, STRIP // 6, send_plain, 0)
+    for e in range(2):
+        edge_ref[e, PLANES] = jnp.zeros((TILE, LANES), F32)
+    send(STRIP // 2, lane ^ 7, 1.0, -1.0)
+    send(STRIP // 2 + 1, lane ^ 7, -1.0, 1.0)
+    send(STRIP // 2 + 2, lane ^ 7, 1.0, 1.0)
 
 
 def interior_kernel(
@@ -437,50 +451,40 @@
 PARAMS = pltpu.CompilerParams(vmem_limit_bytes=40 * 1024 * 1024)
 
 
-def shards(heat, salt, east, north, water, metric_x, metric_y, diffusion, spreading, mirror):
-    rows, cols = metric_x.shape
-    lon_count, lat_count = lax.axis_size("lon"), lax.axis_size("lat")
-    lon, lat = lax.axis_index("lon"), lax.axis_index("lat")
-    lat_info = jnp.stack([lat, jnp.int32(lat_count)]).astype(jnp.int32)
-    pivot = (mirror[0] // cols + lon) % lon_count
-
-    base = (heat, salt, east, north, water, metric_x, metric_y)
-    own, ownx, to_east, to_west = pl.pallas_call(
+def call_pack(base):
+    rows, cols = base[5].shape
+    steps = 2
+    part = rows // steps
+    wide = lambda: pl.BlockSpec((LEVELS, part, cols), lambda i: (0, i, 0))
+    flat = lambda: pl.BlockSpec((part, cols), lambda i: (i, 0))
+    return pl.pallas_call(
         pack_kernel,
+        grid=(steps,),
         out_shape=(shape(2, rows, LANES), shape(3, TILE, LANES), shape(rows + 16, LANES), shape(rows + 16, LANES)),
-        in_specs=vmem(7),
-        out_specs=tuple(vmem(4)),
-        compiler_params=PARAMS,
+        in_specs=[wide() for _ in range(5)] + [flat(), flat()],
+        out_specs=(
+            pl.BlockSpec((2, part, LANES), lambda i: (0, i, 0)),
+            pl.BlockSpec((3, TILE, LANES), lambda i: (0, 0, 0)),
+            pl.BlockSpec((rows + 16, LANES), lambda i: (0, 0)),
+            pl.BlockSpec((rows + 16, LANES), lambda i: (0, 0)),
+        ),
     )(*base)
-    ring = [(i, (i + 1) % lon_count) for i in range(lon_count)]
-    from_west = lax.ppermute(to_east, "lon", ring)
-    from_east = lax.ppermute(to_west, "lon", [(j, i) for i, j in ring])
-    sides = (own, ownx, from_west, from_east)
-
-    rows_a, rows_b, edge = pl.pallas_call(
+
+
+def call_edge(lat_info, base, sides):
+    return pl.pallas_call(
         edge_kernel,
-        out_shape=(shape(PAIRS, TILE, LANES), shape(PAIRS, TILE, LANES), shape(2, PLANES, TILE, LANES)),
+        out_shape=(shape(PAIRS, TILE, LANES), shape(PAIRS, TILE, LANES), shape(2, 2 * PAIRS, TILE, LANES)),
         in_specs=smem(1) + vmem(11),
         out_specs=tuple(vmem(3)),
         compiler_params=PARAMS,
     )(lat_info, *base, *sides)
 
-    index = lambda o, a: o * lat_count + a
-    pairs = [(index(o, a), index(o, a ^ 1)) for o in range(lon_count) for a in range(lat_count)]
-    got_a = lax.ppermute(rows_a, ("lon", "lat"), pairs)
-
-    def across(k, x):
-        fixed = []
-        for o in range(lon_count):
-            for a in range(1, lat_count - 1):
-                fixed.append((index(o, a), index(o, ((a + 1) ^ 1) - 1)))
-            fixed.append((index(o, lat_count - 1), index((k - o) % lon_count, lat_count - 1)))
-        return lax.ppermute(x, ("lon", "lat"), fixed)
-
-    got_b = lax.switch(pivot, [functools.partial(across, k) for k in range(lon_count)], rows_b)
-
+
+def call_interior(spreading, base, diffusion, sides):
+    rows, cols = base[5].shape
     stack_rows = rows + 2 * TILE
-    results = pl.pallas_call(
+    return pl.pallas_call(
         interior_kernel,
         out_shape=(shape(LEVELS, rows, cols),) * 4 + (shape(AD_PLANES, 4 * TILE, LANES), shape(2, 16, TILE, LANES)),
         in_specs=smem(1) + vmem(12),
@@ -496,8 +500,10 @@
         ],
         compiler_params=PARAMS,
     )(spreading, *base, diffusion, *sides)
-    outs, advected, weights = results[:4], results[4], results[5]
-
+
+
+def call_border(lat_info, spreading, diffusion, got_a, got_b, edge, advected, weights, outs):
+    _, rows, cols = outs[0].shape
     last = rows // TILE - 1
     return pl.pallas_call(
         border_kernel,
@@ -524,6 +530,38 @@
     )(lat_info, spreading, diffusion, diffusion, got_a, got_b, edge, advected, weights, *outs)
 
 
+def shards(heat, salt, east, north, water, metric_x, metric_y, diffusion, spreading, mirror):
+    cols = metric_x.shape[1]
+    lon_count, lat_count = lax.axis_size("lon"), lax.axis_size("lat")
+    lon, lat = lax.axis_index("lon"), lax.axis_index("lat")
+    lat_info = jnp.stack([lat, jnp.int32(lat_count)]).astype(jnp.int32)
+    pivot = (mirror[0] // cols + lon) % lon_count
+
+    base = (heat, salt, east, north, water, metric_x, metric_y)
+    own, ownx, to_east, to_west = call_pack(base)
+    ring = [(i, (i + 1) % lon_count) for i in range(lon_count)]
+    from_west = lax.ppermute(to_east, "lon", ring)
+    from_east = lax.ppermute(to_west, "lon", [(j, i) for i, j in ring])
+    sides = (own, ownx, from_west, from_east)
+    rows_a, rows_b, edge = call_edge(lat_info, base, sides)
+
+    index = lambda o, a: o * lat_count + a
+    pairs = [(index(o, a), index(o, a ^ 1)) for o in range(lon_count) for a in range(lat_count)]
+    got_a = lax.ppermute(rows_a, ("lon", "lat"), pairs)
+
+    def across(k, x):
+        fixed = []
+        for o in range(lon_count):
+            for a in range(1, lat_count - 1):
+                fixed.append((index(o, a), index(o, ((a + 1) ^ 1) - 1)))
+            fixed.append((index(o, lat_count - 1), index((k - o) % lon_count, lat_count - 1)))
+        return lax.ppermute(x, ("lon", "lat"), fixed)
+
+    got_b = lax.switch(pivot, [functools.partial(across, k) for k in range(lon_count)], rows_b)
+    results = call_interior(spreading, base, diffusion, sides)
+    return call_border(lat_info, spreading, diffusion, got_a, got_b, edge, results[4], results[5], results[:4])
+
+
 def solution(mesh):
     block = P(None, "lat", "lon")
     in_specs = (block,) * 5 + (P("lat", "lon"),) * 2 + (block, P(), P("lon"))

time: 73.8 us -> 63 us (0.85)
  local copies, waits for them, and re-layouts: 8.34 us -> 1.7 us
  Pallas kernels: 43.8 us -> 39.7 us
    unnamed x38 -> x30, local copies, waits for them, and re-layouts: 8.34 us -> 1.7 us
    pallas_call x4, Pallas kernels: 43.8 us -> 39.7 us  [the longest x1 28.3 us: call_interior(): pl.pallas_call(interior_kernel, out_shape=(shape(LEVELS, rows, cols),) *...]
  transfers between devices with their start and end apart: 4 -> 4, of which waited for: 3 -> 3; matrix products, arithmetic and copies ran while one was open for 0% -> 0% of each run, Pallas kernels for 39% -> 45%
where the time goes in v2:
time: 63 us; the launch traced here: 62.8 us
  Pallas kernels  39.7 us (63%)
  waiting for transfers between devices  10.9 us (17%)
  starting transfers between devices  9.41 us (15%)
  local copies, waits for them, and re-layouts  1.7 us (3%)
  between operations  0.97 us (2%)
    pallas_call x1, Pallas kernels, call_interior(): pl.pallas_call(interior_kernel, out_shape=(shape(LEVELS, rows, cols),) *...  28.3 us
    ppermute x1, waiting for transfers between devices, across(): return lax.ppermute(x, ('lon', 'lat'), fixed)  4.93 us
    pallas_call x1, Pallas kernels, call_pack(): pl.pallas_call(pack_kernel, grid=(steps,), out_shape=(shape(2, rows, LANE...  4.91 us
    ppermute x1, waiting for transfers between devices, shards(): from_east = lax.ppermute(to_west, 'lon', [(j, i) for i, j in ring])  4.37 us
    ppermute x1, starting transfers between devices, across(): return lax.ppermute(x, ('lon', 'lat'), fixed)  4.36 us
    pallas_call x1, Pallas kernels, call_edge(): pl.pallas_call(edge_kernel, out_shape=(shape(PAIRS, TILE, LANES), shape(P...  4.07 us
    ppermute x1, starting transfers between devices, shards(): from_west = lax.ppermute(to_east, 'lon', ring)  3.75 us
    pallas_call x1, Pallas kernels, call_border(): pl.pallas_call(border_kernel, grid=(1,), out_shape=(shape(LEVELS, rows, c...  2.35 us
  transfers between devices with their start and end apart: 4, of which 3 were waited for; matrix products, arithmetic and copies ran while one was open for 0% of the time, Pallas kernels for 45%

profile of v2, /device:TPU:103, one launch (start us, length us, event | category | flops | bytes accessed | tf_op | source)
XLA Modules:
  0.0 62.8 jit_solution(2848486821986365402)
XLA Ops:
  0.6 0.0 copy-start.7
  0.6 0.0 copy-start.6
  0.7 0.0 copy-start.4
  0.7 0.0 copy-start.3
  0.7 0.0 copy-start.2
  0.7 0.0 copy-start.1
  0.7 0.0 copy-start
  0.7 4.9 %shard_map.129 = (f32[2,128,128]{2,1,0:T(8,128)}, f32[3,8,128]{2,1,0:T(8,128)}, f32[144,128]{1,0:T(8,128)}, f32[144,128]{1,0:T(8,128)}) custom-call(f32[8,128,128]{2,1,0:T(8,128)} %t_ref.5, f32[8,128,128]{2,1,0:T(8,128)} %s_ref.5, f32[8,128,128]{2,1,0:T(8,128)} %u_ref.5, f32[8,128,128]{2,1,0:T(8,128)} %v_ref.5, s32[8,128,128]{2,1,0:T(8,128)} %w_ref.5, ...), custom_call_target="tpu_custom_call" | custom-call | tf_op jit(solution)/shard_map/pallas_call | solution.py:460
  5.6 3.8 %collective-permute-start.32 = (f32[144,128]{1,0:T(8,128)}, f32[144,128]{1,0:T(8,128)S(1)}, u32[]{:S(2)}, u32[]{:S(2)}) collective-permute-start(f32[144,128]{1,0:T(8,128)} %get-tuple-element.84), channel_id=1, source_target_pairs={{0,8},{8,16},{16,24},{24,32},{32,40},{40,48},{48,56},{56,64},{64,7... | collective-permute-start | bytes 221192 | tf_op jit(solution)/shard_map/ppermute | solution.py:543
  9.4 0.0 collective-permute-start.33
  9.4 0.1 pad_add_fusion.lat_ref
  9.5 1.6 %collective-permute-done.32.fromw_ref = f32[144,128]{1,0:T(8,128)S(1)} collective-permute-done((f32[144,128]{1,0:T(8,128)}, f32[144,128]{1,0:T(8,128)S(1)}, u32[]{:S(2)}, u32[]{:S(2)}) %collective-permute-start.32) | collective-permute-done | bytes 73760 | tf_op jit(solution)/shard_map/ppermute | solution.py:543
  11.1 4.4 %collective-permute-done.33.frome_ref = f32[144,128]{1,0:T(8,128)S(1)} collective-permute-done((f32[144,128]{1,0:T(8,128)}, f32[144,128]{1,0:T(8,128)S(1)}, u32[]{:S(2)}, u32[]{:S(2)}) %collective-permute-start.33) | collective-permute-done | bytes 73760 | tf_op jit(solution)/shard_map/ppermute | solution.py:544
  15.5 0.0 copy-done.7
  15.5 0.0 copy-done.6
  15.5 0.0 copy-done.4
  15.5 0.0 copy-done.3
  15.5 0.0 copy-done.2
  15.5 0.0 copy-done.1
  15.5 0.0 copy-done
  15.5 0.0 copy-start.8
  15.5 0.9 %copy-done.8 = f32[2,128,128]{2,1,0:T(8,128)S(1)} copy-done((f32[2,128,128]{2,1,0:T(8,128)S(1)}, f32[2,128,128]{2,1,0:T(8,128)}, u32[]{:S(2)}) %copy-start.8) | copy-done | bytes 131096
  16.4 4.1 %shard_map.130 = (f32[24,8,128]{2,1,0:T(8,128)}, f32[24,8,128]{2,1,0:T(8,128)}, f32[2,48,8,128]{3,2,1,0:T(8,128)S(1)}) custom-call(s32[2]{0:T(128)S(1)} %pad_add_fusion.lat_ref, f32[8,128,128]{2,1,0:T(8,128)S(1)} %copy-done, f32[8,128,128]{2,1,0:T(8,128)S(1)} %copy-done.1, f32[8,128,128]{2,1,0:T(8,128)S(1)} %copy-done.2, f32[8,128,128]{2,1,0:T(8,128)S(1)} %copy-done.3, ...), custom_call_target="tpu_custom_call" | custom-call | tf_op jit(solution)/shard_map/pallas_call | solution.py:475
  20.5 0.7 %copy-done.10 = f32[2,48,8,128]{3,2,1,0:T(8,128)} copy-done((f32[2,48,8,128]{3,2,1,0:T(8,128)}, f32[2,48,8,128]{3,2,1,0:T(8,128)S(1)}, u32[]{:S(2)}) %copy-start.10) | copy-done | bytes 393240
  21.3 1.3 %collective-permute-start.34 = (f32[24,8,128]{2,1,0:T(8,128)}, f32[24,8,128]{2,1,0:T(8,128)}, u32[]{:S(2)}, u32[]{:S(2)}) collective-permute-start(f32[24,8,128]{2,1,0:T(8,128)} %get-tuple-element.86), channel_id=1, source_target_pairs={{0,1},{1,0},{2,3},{3,2},{4,5},{5,4},{6,7},{7,6},{8,9},{9,8},{10,11... | collective-permute-start | bytes 294920 | tf_op jit(solution)/shard_map/ppermute | solution.py:550
  22.8 9.3 %conditional.1 = (f32[24,8,128]{2,1,0:T(8,128)}) conditional(s32[]{:T(128)} %clamp.3, f32[24,8,128]{2,1,0:T(8,128)} %get-tuple-element.87, f32[24,8,128]{2,1,0:T(8,128)} %get-tuple-element.87, f32[24,8,128]{2,1,0:T(8,128)} %get-tuple-element.87, f32[24,8,128]{2,1,0:T(8,128)} %get-tuple-element.87, ...), branch_computations={%region_0.1_spmd, %region_1.2_spmd, %region_2.3_spmd, %region_3.4_... | conditional | bytes 393264 | solution.py:560
  22.8 4.4 %collective-permute-start.10 = (f32[24,8,128]{2,1,0:T(8,128)}, f32[24,8,128]{2,1,0:T(8,128)}, u32[]{:S(2)}, u32[]{:S(2)}) collective-permute-start(f32[24,8,128]{2,1,0:T(8,128)} %param.10), channel_id=1, source_target_pairs={{1,2},{2,1},{3,4},{4,3},{5,6},{6,5},{7,87},{9,10},{10,9},{11,12},{... | collective-permute-start | bytes 294920 | tf_op jit(solution)/shard_map/cond/branch_10_fun/ppermute | solution.py:558
  27.1 4.9 %collective-permute-done.10 = f32[24,8,128]{2,1,0:T(8,128)} collective-permute-done((f32[24,8,128]{2,1,0:T(8,128)}, f32[24,8,128]{2,1,0:T(8,128)}, u32[]{:S(2)}, u32[]{:S(2)}) %collective-permute-start.10) | collective-permute-done | bytes 98336 | tf_op jit(solution)/shard_map/cond/branch_10_fun/ppermute | solution.py:558
  32.1 0.0 copy-start.11
  32.1 28.3 %shard_map.131 = (f32[8,128,128]{2,1,0:T(8,128)}, f32[8,128,128]{2,1,0:T(8,128)}, f32[8,128,128]{2,1,0:T(8,128)}, f32[8,128,128]{2,1,0:T(8,128)}, f32[42,32,128]...) custom-call(f32[4,8]{1,0:T(4,128)S(1)} %copy-done.13, f32[8,128,128]{2,1,0:T(8,128)S(1)} %copy-done, ...), custom_call_target="tpu_custom_call" | custom-call | tf_op jit(solution)/shard_map/pallas_call | solution.py:487
  60.4 0.0 collective-permute-done.34.a_ref
  60.5 2.3 %shard_map.132 = (f32[8,128,128]{2,1,0:T(8,128)}, f32[8,128,128]{2,1,0:T(8,128)}, f32[8,128,128]{2,1,0:T(8,128)}, f32[8,128,128]{2,1,0:T(8,128)}) custom-call(s32[2]{0:T(128)S(1)} %pad_add_fusion.lat_ref, f32[4,8]{1,0:T(4,128)S(1)} %copy-done.13, ...), custom_call_target="tpu_custom_call", output_to_operand_aliasing={{0}: (9, {}), {1}: (10, {}), {2}: (11, {}), {3}: (12, {})} | custom-call | tf_op jit(solution)/shard_map/pallas_call | solution.py:508
  (12 shorter events, 0.0 us)
Async XLA Ops:
  0.6 14.8 %copy-start.7 = (f32[128,128]{1,0:T(8,128)S(1)}, f32[128,128]{1,0:T(8,128)}, u32[]{:S(2)}) copy-start(f32[128,128]{1,0:T(8,128)} %my_ref.5) | copy-start | bytes 196612
  0.6 14.8 %copy-start.6 = (f32[128,128]{1,0:T(8,128)S(1)}, f32[128,128]{1,0:T(8,128)}, u32[]{:S(2)}) copy-start(f32[128,128]{1,0:T(8,128)} %mx_ref.5) | copy-start | bytes 196612
  0.7 14.8 %copy-start.4 = (s32[8,128,128]{2,1,0:T(8,128)S(1)}, s32[8,128,128]{2,1,0:T(8,128)}, u32[]{:S(2)}) copy-start(s32[8,128,128]{2,1,0:T(8,128)} %w_ref.5) | copy-start | bytes 1572868
  0.7 14.8 %copy-start.3 = (f32[8,128,128]{2,1,0:T(8,128)S(1)}, f32[8,128,128]{2,1,0:T(8,128)}, u32[]{:S(2)}) copy-start(f32[8,128,128]{2,1,0:T(8,128)} %v_ref.5) | copy-start | bytes 1572868
  0.7 14.8 %copy-start.2 = (f32[8,128,128]{2,1,0:T(8,128)S(1)}, f32[8,128,128]{2,1,0:T(8,128)}, u32[]{:S(2)}) copy-start(f32[8,128,128]{2,1,0:T(8,128)} %u_ref.5) | copy-start | bytes 1572868
  0.7 14.8 %copy-start.1 = (f32[8,128,128]{2,1,0:T(8,128)S(1)}, f32[8,128,128]{2,1,0:T(8,128)}, u32[]{:S(2)}) copy-start(f32[8,128,128]{2,1,0:T(8,128)} %s_ref.5) | copy-start | bytes 1572868
  0.7 14.8 %copy-start = (f32[8,128,128]{2,1,0:T(8,128)S(1)}, f32[8,128,128]{2,1,0:T(8,128)}, u32[]{:S(2)}) copy-start(f32[8,128,128]{2,1,0:T(8,128)} %t_ref.5) | copy-start | bytes 1572868
  5.6 9.9 %copy-start.12 = (f32[3,8,128]{2,1,0:T(8,128)S(1)}, f32[3,8,128]{2,1,0:T(8,128)}, u32[]{:S(2)}) copy-start(f32[3,8,128]{2,1,0:T(8,128)} %get-tuple-element.83.ownx_ref) | copy-start | bytes 36868
  5.6 5.5 %collective-permute-start.32 = (f32[144,128]{1,0:T(8,128)}, f32[144,128]{1,0:T(8,128)S(1)}, u32[]{:S(2)}, u32[]{:S(2)}) collective-permute-start(f32[144,128]{1,0:T(8,128)} %get-tuple-element.84), channel_id=1, source_target_pairs={{0,8},{8,16},{16,24},{24,32},{32,40},{40,48},{48,56},{56,64},{64,7... | collective-permute-start | bytes 221192 | tf_op jit(solution)/shard_map/ppermute | solution.py:543
  9.4 6.1 %collective-permute-start.33 = (f32[144,128]{1,0:T(8,128)}, f32[144,128]{1,0:T(8,128)S(1)}, u32[]{:S(2)}, u32[]{:S(2)}) collective-permute-start(f32[144,128]{1,0:T(8,128)} %get-tuple-element.85), channel_id=1, source_target_pairs={{8,0},{16,8},{24,16},{32,24},{40,32},{48,40},{56,48},{64,56},{72,6... | collective-permute-start | bytes 221192 | tf_op jit(solution)/shard_map/ppermute | solution.py:544
  15.5 0.9 %copy-start.8 = (f32[2,128,128]{2,1,0:T(8,128)S(1)}, f32[2,128,128]{2,1,0:T(8,128)}, u32[]{:S(2)}) copy-start(f32[2,128,128]{2,1,0:T(8,128)} %get-tuple-element.82.own_ref) | copy-start | bytes 393220
  16.4 6.1 %copy-start.14 = (s32[128]{0:T(128)S(1)}, s32[128]{0:T(128)}, u32[]{:S(2)}) copy-start(s32[128]{0:T(128)} %param.51) | copy-start | bytes 1540
  16.4 15.6 %copy-start.5 = (f32[7,128,128]{2,1,0:T(8,128)S(1)}, f32[7,128,128]{2,1,0:T(8,128)}, u32[]{:S(2)}) copy-start(f32[7,128,128]{2,1,0:T(8,128)} %idf_hi.1) | copy-start | bytes 1376260
  16.4 15.6 %copy-start.13 = (f32[4,8]{1,0:T(4,128)S(1)}, f32[4,8]{1,0:T(4,128)}, u32[]{:S(2)}) copy-start(f32[4,8]{1,0:T(4,128)} %coef_ref.3) | copy-start | bytes 388
  20.5 0.8 %copy-start.10 = (f32[2,48,8,128]{3,2,1,0:T(8,128)}, f32[2,48,8,128]{3,2,1,0:T(8,128)S(1)}, u32[]{:S(2)}) copy-start(f32[2,48,8,128]{3,2,1,0:T(8,128)S(1)} %get-tuple-element.88.edge_ref) | copy-start | bytes 1179652
  21.3 10.8 %copy-start.9 = (f32[2,128,128]{2,1,0:T(8,128)S(1)}, f32[2,128,128]{2,1,0:T(8,128)}, u32[]{:S(2)}) copy-start(f32[2,128,128]{2,1,0:T(8,128)} %get-tuple-element.82.own_ref) | copy-start | bytes 393220
  21.3 39.2 %collective-permute-start.34 = (f32[24,8,128]{2,1,0:T(8,128)}, f32[24,8,128]{2,1,0:T(8,128)}, u32[]{:S(2)}, u32[]{:S(2)}) collective-permute-start(f32[24,8,128]{2,1,0:T(8,128)} %get-tuple-element.86), channel_id=1, source_target_pairs={{0,1},{1,0},{2,3},{3,2},{4,5},{5,4},{6,7},{7,6},{8,9},{9,8},{10,11... | collective-permute-start | bytes 294920 | tf_op jit(solution)/shard_map/ppermute | solution.py:550
  22.8 9.3 %collective-permute-start.10 = (f32[24,8,128]{2,1,0:T(8,128)}, f32[24,8,128]{2,1,0:T(8,128)}, u32[]{:S(2)}, u32[]{:S(2)}) collective-permute-start(f32[24,8,128]{2,1,0:T(8,128)} %param.10), channel_id=1, source_target_pairs={{1,2},{2,1},{3,4},{4,3},{5,6},{6,5},{7,87},{9,10},{10,9},{11,12},{... | collective-permute-start | bytes 294920 | tf_op jit(solution)/shard_map/cond/branch_10_fun/ppermute | solution.py:558
  32.1 28.4 %copy-start.11 = (f32[2,48,8,128]{3,2,1,0:T(8,128)S(1)}, f32[2,48,8,128]{3,2,1,0:T(8,128)}, u32[]{:S(2)}) copy-start(f32[2,48,8,128]{3,2,1,0:T(8,128)} %copy-done.10) | copy-start | bytes 1179652

commit v3 on v2

--- a/solution.py
+++ b/solution.py
@@ -12,7 +12,8 @@
 LANES = 128
 VM, DEPTH, METRIC, STRIP, VM_S, DEPTH_S, METRIC_S, PLANES = 32, 40, 41, 42, 44, 45, 46, 47
 PAIRS = 24
-AD_STRIP, WY, AD_PLANES = 32, 34, 42
+FACES, TURNED = 37, 44
+AD_STRIP, WY, AD_PLANES = 32, 34, 36
 
 
 def roll(x, shift):
@@ -44,10 +45,10 @@
     return own * edge + centre * jnp.where(positive, here, after) - far * jnp.where(positive, edge_before, edge_after)
 
 
-def pack_kernel(t_ref, s_ref, u_ref, v_ref, w_ref, mx_ref, my_ref, own_ref, ownx_ref, toe_ref, tow_ref):
+def pack_kernel(t_ref, s_ref, u_ref, v_ref, w_ref, mx_ref, my_ref, own_ref, ownx_ref, toe_ref, tow_ref, depths):
     fields = (t_ref, s_ref, u_ref, v_ref)
-    step, tiles = pl.program_id(0), mx_ref.shape[0] // TILE
-    rows_total = toe_ref.shape[0] - 2 * TILE
+    step, tiles = pl.program_id(0), t_ref.shape[1] // TILE
+    rows_total = mx_ref.shape[0]
     lane = iota(1)
     low = (lane & 7) < 4
     group = lane >> 3
@@ -75,7 +76,8 @@
         toe_ref[whole, :] = jnp.where(low, packs[0], roll(packs[1], 4))
         tow_ref[whole, :] = jnp.where(low, roll(packs[1], -4), packs[0])
         shift = (4 + 8 * tile) & (LANES - 1)
-        for i, x in enumerate((depth, mx_ref[rows, :], my_ref[rows, :])):
+        depths[whole, :] = depth
+        for i, x in enumerate((depth, mx_ref[whole, :], my_ref[whole, :])):
             ownx_ref[i] = jnp.where(group == tile, pltpu.roll(x, shift, 1), ownx_ref[i])
         return carry
 
@@ -89,9 +91,18 @@
         toe_ref[second, :] = jnp.where(low, metric_y, 0.0)
         tow_ref[first, :] = jnp.where(low, roll(metric_x, -4), depth)
         tow_ref[second, :] = jnp.where(low, 0.0, metric_y)
-
-
-def x_tile(t, fields, w_ref, mx_ref, my_ref, own_ref, ownx_ref, fromw_ref, frome_ref, put, put_weight):
+        upper = iota(0) < 4
+        turned = [x[...].T for x in (depths, mx_ref, my_ref)]
+        starts = [x[:TILE] for x in turned]
+        ends = [x[-TILE:] for x in turned]
+        third, fourth = pl.ds(rows_total + 2 * TILE, TILE), pl.ds(rows_total + 3 * TILE, TILE)
+        toe_ref[third, :] = jnp.where(upper, turn(ends[0], 4), ends[1])
+        tow_ref[third, :] = jnp.where(upper, starts[1], turn(starts[0], 4))
+        toe_ref[fourth, :] = jnp.where(upper, turn(ends[2], 4), 0.0)
+        tow_ref[fourth, :] = jnp.where(upper, 0.0, turn(starts[2], 4))
+
+
+def x_tile(t, fields, w_ref, mx_ref, my_ref, own_ref, ownx_ref, fromw_ref, frome_ref, put):
     rows_total = mx_ref.shape[0]
     start = pl.multiple_of(t * TILE, TILE)
     rows = pl.ds(start, TILE)
@@ -125,7 +136,7 @@
         extra.append((spread(jnp.where(low, side_halo[i], mine)), spread(jnp.where(low, mine, side_halo[i]))))
     depth_s, mx_s, my_s = extra
 
-    um_s, weight_s, edge_s, flux_s, star_s, vm_s = [], [], [[], []], [[], []], [[], []], []
+    um_s, edge_s, flux_s, star_s, vm_s = [], [[], []], [[], []], [[], []], []
     for side in range(2):
         mixed = strips[1][side]
         swapped = roll(mixed, 64)
@@ -134,7 +145,6 @@
         opening = jnp.minimum(depth_s[side], roll(depth_s[side], -1)) > level
         coefs = face_coefs(jnp.where(opening, 0.5 * (um + roll(um, -1)), 0.0))
         um_s.append(um)
-        weight_s.append(jnp.where(opening, 0.5 * (mx_s[side] + roll(mx_s[side], -1)), 0.0))
         for k in range(2):
             q = strips[k][side]
             after = roll(q, -1)
@@ -158,7 +168,6 @@
     put(DEPTH, depth)
     put(METRIC, my)
     shallow = jnp.minimum(depth, roll(jnp.where(head, roll(depth_s[1], -4), depth), -1))
-    mean_metric = 0.5 * (mx + roll(jnp.where(head, roll(mx_s[1], -4), mx), -1))
     for l in range(LEVELS):
         masked = [jnp.where(wet[l] != 0, field[l, rows, :], 0.0) for field in fields]
         um = masked[2] * mx
@@ -168,10 +177,6 @@
         coefs = face_coefs(
             jnp.where(opening, 0.5 * (um + roll(jnp.where(head, roll(um_halo, place), um), -1)), 0.0)
         )
-        if put_weight is not None:
-            weight = jnp.where(opening, mean_metric, 0.0)
-            put_weight(l, weight)
-            put_weight(LEVELS + l, roll(jnp.where(tail, roll(weight_s[0], place), weight), 1))
         for f in range(4):
             q, k = masked[f], f // 2
             place = 124 - 8 * ((f % 2) * 8 + l)
@@ -191,12 +196,13 @@
             put(f * LEVELS + l, q + roll(jnp.where(tail, h, flux), 1) - flux)
 
 
-def field_planes():
-    return [(p, p) for p in range(32)] + [(STRIP, AD_STRIP), (STRIP + 1, AD_STRIP + 1)]
-
-
-def y_edges(stack, edges, r):
-    for p, to in field_planes():
+def field_planes(strips):
+    planes = [(p, p) for p in range(32)]
+    return planes + [(STRIP, AD_STRIP), (STRIP + 1, AD_STRIP + 1)] if strips else planes
+
+
+def all_edges(stack, edges, r, strips=True):
+    for p, to in field_planes(strips):
         edges[to, pl.ds(r, TILE), :] = edge_sum(
             stack[p, pl.ds(r - 1, TILE), :],
             stack[p, pl.ds(r, TILE), :],
@@ -205,7 +211,7 @@
         )
 
 
-def y_fluxes(stack, edges, fluxes, advected, r):
+def all_fluxes(stack, edges, fluxes, r, put_weight, strips=True):
     here, after = pl.ds(r, TILE), pl.ds(r + 1, TILE)
 
     def put(coefs, p, to):
@@ -220,29 +226,40 @@
 
     shallow = jnp.minimum(stack[DEPTH, here, :], stack[DEPTH, after, :])
     mean_metric = 0.5 * (stack[METRIC, here, :] + stack[METRIC, after, :])
+    put_weight(shallow, mean_metric)
     for l in range(LEVELS):
         opening = shallow > float(l)
         coefs = face_coefs(jnp.where(opening, 0.5 * (stack[VM + l, here, :] + stack[VM + l, after, :]), 0.0))
-        advected[WY + l, here, :] = jnp.where(opening, mean_metric, 0.0)
         for f in range(4):
             put(coefs, f * LEVELS + l, f * LEVELS + l)
-    level = ((iota(1) >> 3) & 7).astype(F32)
-    opening = jnp.minimum(stack[DEPTH_S, here, :], stack[DEPTH_S, after, :]) > level
-    coefs = face_coefs(jnp.where(opening, 0.5 * (stack[VM_S, here, :] + stack[VM_S, after, :]), 0.0))
-    for k in range(2):
-        put(coefs, STRIP + k, AD_STRIP + k)
-
-
-def y_updates(stack, fluxes, advected, r):
+    if strips:
+        level = ((iota(1) >> 3) & 7).astype(F32)
+        opening = jnp.minimum(stack[DEPTH_S, here, :], stack[DEPTH_S, after, :]) > level
+        coefs = face_coefs(jnp.where(opening, 0.5 * (stack[VM_S, here, :] + stack[VM_S, after, :]), 0.0))
+        for k in range(2):
+            put(coefs, STRIP + k, AD_STRIP + k)
+
+
+def all_updates(stack, fluxes, advected, r, strips=True):
     here, before = pl.ds(r, TILE), pl.ds(r - 1, TILE)
-    for p, to in field_planes():
+    for p, to in field_planes(strips):
         advected[to, here, :] = stack[p, here, :] + fluxes[to, before, :] - fluxes[to, here, :]
+
+
+def weights_to(ref, r, at=0):
+    def put(shallow, mean_metric):
+        ref[at, pl.ds(r, TILE), :] = shallow
+        ref[at + 1, pl.ds(r, TILE), :] = mean_metric
+
+    return put
 
 
 def finish(advected, r, depth, weights, coupling, spreading, put):
     lane = iota(1)
     head, tail = lane == 0, lane == LANES - 1
     here, before, after = pl.ds(r, TILE), pl.ds(r - 1, TILE), pl.ds(r + 1, TILE)
+    face = [(weights(0), weights(1)), (weights(2), weights(3))]
+    face += [(advected[WY, at, :], advected[WY + 1, at, :]) for at in (here, before)]
     links, factors, inverses = [], [], []
     for l in range(LEVELS):
         divisor = jnp.ones((TILE, LANES), F32)
@@ -258,13 +275,14 @@
         reduced = []
         for l in range(LEVELS):
             p = f * LEVELS + l
+            x_up, x_down, y_up, y_down = (jnp.where(shallow > float(l), mean, 0.0) for shallow, mean in face)
             a = advected[p, here, :]
             h = roll(advected[AD_STRIP + f // 2, here, :], 124 - 8 * ((f % 2) * 8 + l))
             bend = (
-                weights(l) * (roll(jnp.where(head, h, a), -1) - a)
-                - weights(LEVELS + l) * (a - roll(jnp.where(tail, h, a), 1))
-                + advected[WY + l, here, :] * (advected[p, after, :] - a)
-                - advected[WY + l, before, :] * (a - advected[p, before, :])
+                x_up * (roll(jnp.where(head, h, a), -1) - a)
+                - x_down * (a - roll(jnp.where(tail, h, a), 1))
+                + y_up * (advected[p, after, :] - a)
+                - y_down * (a - advected[p, before, :])
             )
             target = a + spreading[f, l] * bend
             if l > 0:
@@ -288,7 +306,7 @@
         def put(p, x):
             edge_ref[e, p] = x
 
-        x_tile(e * (tiles - 1), fields, w_ref, mx_ref, my_ref, own_ref, ownx_ref, fromw_ref, frome_ref, put, None)
+        x_tile(e * (tiles - 1), fields, w_ref, mx_ref, my_ref, own_ref, ownx_ref, fromw_ref, frome_ref, put)
         return carry
 
     lax.fori_loop(0, 2, sweep, 0)
@@ -323,36 +341,121 @@
     send(STRIP // 2 + 2, lane ^ 7, 1.0, 1.0)
 
 
+def flip_kernel(t_ref, s_ref, u_ref, v_ref, w_ref, mx_ref, turned_ref, side_ref):
+    fields = (t_ref, s_ref, u_ref, v_ref)
+
+    def body(l, carry):
+        wet = w_ref[l]
+        for f in range(4):
+            turned_ref[f * LEVELS + l] = jnp.where(wet != 0, fields[f][l], 0.0).T
+        return carry + wet
+
+    depth = lax.fori_loop(0, LEVELS, body, jnp.zeros(mx_ref.shape, jnp.int32))
+    side_ref[0] = depth.astype(F32).T
+    side_ref[1] = mx_ref[...].T
+
+
 def interior_kernel(
-    coef_ref, t_ref, s_ref, u_ref, v_ref, w_ref, mx_ref, my_ref, idf_ref, own_ref, ownx_ref, fromw_ref, frome_ref,
+    coef_ref, turned_ref, side_ref, v_ref, w_ref, my_ref, idf_ref, fromw_ref, frome_ref,
     o0, o1, o2, o3, adv_ref, weight_ref,
-    stack, edges, fluxes, advected, weights, out, sems,
+    wide, edges, fluxes, wide_star, halos, stack, advected, out, sems,
 ):
-    fields = (t_ref, s_ref, u_ref, v_ref)
     outs = (o0, o1, o2, o3)
-    rows_total = mx_ref.shape[0]
-    tiles = rows_total // TILE
-
-    def sweep_x(t, carry):
+    rows_total, cols_total = my_ref.shape
+    tiles, col_tiles = rows_total // TILE, cols_total // TILE
+    margin = 2 * TILE
+    inner = pl.ds(margin, cols_total)
+    sub = iota(0)
+    upper = sub < 4
+    lane = lax.broadcasted_iota(jnp.int32, (rows_total, LANES), 1)
+    low = (lane & 7) < 4
+    every = pl.ds(0, rows_total)
+    west, east = fromw_ref[every, :], frome_ref[every, :]
+    for k, halo in enumerate((jnp.where(low, west, east), jnp.where(low, roll(west, -4), roll(east, 4)))):
+        halos[pl.ds(k * 16, 16)] = halo.T.reshape(16, TILE, rows_total)
+    third, fourth = pl.ds(rows_total + 2 * TILE, TILE), pl.ds(rows_total + 3 * TILE, TILE)
+    depth_halo = jnp.where(upper, fromw_ref[third, :], frome_ref[third, :])
+    mx_halo = jnp.where(upper, turn(fromw_ref[third, :], 4), turn(frome_ref[third, :], 4))
+    my_halo = jnp.where(upper, fromw_ref[fourth, :], frome_ref[fourth, :])
+
+    def fill(p, middle, halo):
+        halo = turn(halo, 4)
+        wide[p, pl.ds(TILE, TILE), :] = halo
+        wide[p, pl.ds(margin + cols_total, TILE), :] = halo
+        wide[p, inner, :] = middle
+
+    def fill_field(p, carry):
+        fill(p, turned_ref[p], halos[p])
+        return carry
+
+    lax.fori_loop(0, 32, fill_field, 0)
+    fill(DEPTH, side_ref[0], depth_halo)
+    fill(METRIC, side_ref[1], mx_halo)
+
+    def sweep_wide_edges(j, carry):
+        r = pl.multiple_of(j * TILE, TILE)
+        here = pl.ds(r, TILE)
+        metric = wide[METRIC, here, :]
+        for l in range(LEVELS):
+            wide[VM + l, here, :] = wide[2 * LEVELS + l, here, :] * metric
+        all_edges(wide, edges, r, False)
+        return carry
+
+    def sweep_wide(j, carry):
+        r = pl.multiple_of(j * TILE, TILE)
+
+        def put(shallow, mean_metric):
+            for k, at in enumerate((r, r + 1)):
+                wide_star[FACES + 2 * k, pl.ds(at, TILE), :] = shallow
+                wide_star[FACES + 2 * k + 1, pl.ds(at, TILE), :] = mean_metric
+
+        all_fluxes(wide, edges, fluxes, r, put, False)
+        all_updates(wide, fluxes, wide_star, r, False)
+        return carry
+
+    lax.fori_loop(1, col_tiles + 3, sweep_wide_edges, 0)
+    lax.fori_loop(1, col_tiles + 3, sweep_wide, 0)
+
+    def sweep_strips(p, carry):
+        rows = pl.ds(pl.multiple_of(margin + p * TILE, TILE), TILE)
+        for k in range(2):
+            left = wide_star[p + 16 * k, pl.ds(TILE, TILE), :]
+            right = wide_star[p + 16 * k, pl.ds(margin + cols_total, TILE), :]
+            wide_star[32 + k, rows, :] = jnp.where(sub == 3, turn(left, 4), turn(right, 4))
+        wide_star[34, rows, :] = halos[3 * LEVELS + (p & 7)] * my_halo
+        wide_star[35, rows, :] = depth_halo
+        wide_star[36, rows, :] = my_halo
+        return carry
+
+    lax.fori_loop(0, 16, sweep_strips, 0)
+    body_rows = pl.ds(TILE, rows_total)
+
+    def sweep_back(i, carry):
+        for k in range(4):
+            p = i * 4 + k
+            stack[p + (STRIP - 32) * (p >= 32).astype(jnp.int32), body_rows, :] = wide_star[p, inner, :].T
+        return carry
+
+    lax.fori_loop(0, TURNED // 4, sweep_back, 0)
+
+    def sweep_own(t, carry):
         start = pl.multiple_of(t * TILE, TILE)
-
-        def put(p, x):
-            stack[p, pl.ds(start + TILE, TILE), :] = x
-
-        def put_weight(p, x):
-            weights[p, pl.ds(start, TILE), :] = x
-
-        x_tile(t, fields, w_ref, mx_ref, my_ref, own_ref, ownx_ref, fromw_ref, frome_ref, put, put_weight)
-        return carry
-
-    def sweep_edges(t, carry):
-        y_edges(stack, edges, pl.multiple_of(t * TILE + TILE, TILE))
+        rows, here = pl.ds(start, TILE), pl.ds(start + TILE, TILE)
+        my = my_ref[rows, :]
+        depth = w_ref[0, rows, :]
+        for l in range(1, LEVELS):
+            depth = depth + w_ref[l, rows, :]
+        stack[DEPTH, here, :] = depth.astype(F32)
+        stack[METRIC, here, :] = my
+        for l in range(LEVELS):
+            stack[VM + l, here, :] = jnp.where(w_ref[l, rows, :] != 0, v_ref[l, rows, :], 0.0) * my
+        all_edges(stack, edges, start + TILE)
         return carry
 
     def sweep_y(t, carry):
         r = pl.multiple_of(t * TILE + TILE, TILE)
-        y_fluxes(stack, edges, fluxes, advected, r)
-        y_updates(stack, fluxes, advected, r)
+        all_fluxes(stack, edges, fluxes, r, weights_to(advected, r, WY))
+        all_updates(stack, fluxes, advected, r)
         return carry
 
     def copies(t_rows):
@@ -371,20 +474,19 @@
 
         finish(
             advected, pl.multiple_of(start + TILE, TILE), depth,
-            lambda p: weights[p, rows, :], lambda l: idf_ref[l, rows, :], coef_ref, put,
+            lambda i: stack[PLANES + i, pl.ds(start + TILE, TILE), :], lambda l: idf_ref[l, rows, :], coef_ref, put,
         )
         for copy in copies(rows):
             copy.start()
         return carry
 
-    lax.fori_loop(0, tiles, sweep_x, 0)
-    lax.fori_loop(0, tiles, sweep_edges, 0)
+    lax.fori_loop(0, tiles, sweep_own, 0)
     lax.fori_loop(0, tiles, sweep_y, 0)
     lax.fori_loop(1, tiles - 1, sweep_out, 0)
     for e, start in enumerate((0, rows_total - 2 * TILE)):
         adv_ref[:, pl.ds(e * 2 * TILE, 2 * TILE), :] = advected[:, pl.ds(start + TILE, 2 * TILE), :]
     for e, start in enumerate((0, rows_total - TILE)):
-        weight_ref[e] = weights[:, pl.ds(start, TILE), :]
+        weight_ref[e] = stack[pl.ds(PLANES, 4), pl.ds(start + TILE, TILE), :]
     for copy in copies(pl.ds(TILE, rows_total - 2 * TILE)):
         copy.wait()
 
@@ -409,9 +511,10 @@
                 stack[p, pl.ds(2 * TILE, TILE), :] = halo if p % 2 == 0 else turn(halo, 4)
             stack[p, pl.ds(TILE, TILE), :] = edge_ref[e, p]
         advected[:, pl.ds(TILE if e == 0 else 0, 2 * TILE), :] = adv_ref[:, pl.ds(e * 2 * TILE, 2 * TILE), :]
-        y_edges(stack, edges, 5 if e == 0 else 11)
-        y_fluxes(stack, edges, fluxes, advected, 6 if e == 0 else 12)
-        y_updates(stack, fluxes, advected, 3 if e == 0 else 13)
+        all_edges(stack, edges, 5 if e == 0 else 11)
+        face = 6 if e == 0 else 12
+        all_fluxes(stack, edges, fluxes, face, weights_to(advected, face, WY))
+        all_updates(stack, fluxes, advected, 3 if e == 0 else 13)
 
         def put(p, x, e=e):
             out[e, p] = x
@@ -456,17 +559,18 @@
     steps = 2
     part = rows // steps
     wide = lambda: pl.BlockSpec((LEVELS, part, cols), lambda i: (0, i, 0))
-    flat = lambda: pl.BlockSpec((part, cols), lambda i: (i, 0))
+    flat = lambda: pl.BlockSpec((rows, cols), lambda i: (0, 0))
     return pl.pallas_call(
         pack_kernel,
         grid=(steps,),
-        out_shape=(shape(2, rows, LANES), shape(3, TILE, LANES), shape(rows + 16, LANES), shape(rows + 16, LANES)),
+        out_shape=(shape(2, rows, LANES), shape(3, TILE, LANES), shape(rows + 4 * TILE, LANES), shape(rows + 4 * TILE, LANES)),
         in_specs=[wide() for _ in range(5)] + [flat(), flat()],
+        scratch_shapes=[pltpu.VMEM((rows, LANES), F32)],
         out_specs=(
             pl.BlockSpec((2, part, LANES), lambda i: (0, i, 0)),
             pl.BlockSpec((3, TILE, LANES), lambda i: (0, 0, 0)),
-            pl.BlockSpec((rows + 16, LANES), lambda i: (0, 0)),
-            pl.BlockSpec((rows + 16, LANES), lambda i: (0, 0)),
+            pl.BlockSpec((rows + 4 * TILE, LANES), lambda i: (0, 0)),
+            pl.BlockSpec((rows + 4 * TILE, LANES), lambda i: (0, 0)),
         ),
     )(*base)
 
@@ -481,25 +585,40 @@
     )(lat_info, *base, *sides)
 
 
-def call_interior(spreading, base, diffusion, sides):
+def call_flip(base):
     rows, cols = base[5].shape
+    return pl.pallas_call(
+        flip_kernel,
+        out_shape=(shape(32, cols, rows), shape(2, cols, rows)),
+        in_specs=vmem(6),
+        out_specs=tuple(vmem(2)),
+        compiler_params=PARAMS,
+        cost_estimate=pl.CostEstimate(flops=8_000_000, bytes_accessed=5_000_000, transcendentals=0),
+    )(*base[:6])
+
+
+def call_interior(spreading, turned, side, north, water, metric_y, diffusion, from_west, from_east):
+    rows, cols = metric_y.shape
     stack_rows = rows + 2 * TILE
+    wide_rows = cols + 4 * TILE
     return pl.pallas_call(
         interior_kernel,
-        out_shape=(shape(LEVELS, rows, cols),) * 4 + (shape(AD_PLANES, 4 * TILE, LANES), shape(2, 16, TILE, LANES)),
-        in_specs=smem(1) + vmem(12),
+        out_shape=(shape(LEVELS, rows, cols),) * 4 + (shape(AD_PLANES, 4 * TILE, LANES), shape(2, 4, TILE, LANES)),
+        in_specs=smem(1) + vmem(8),
         out_specs=tuple(anywhere(4) + vmem(2)),
         scratch_shapes=[
-            pltpu.VMEM((PLANES, stack_rows, LANES), F32),
-            pltpu.VMEM((34, stack_rows, LANES), F32),
-            pltpu.VMEM((34, stack_rows, LANES), F32),
+            pltpu.VMEM((STRIP, wide_rows, rows), F32),
+            pltpu.VMEM((34, wide_rows, LANES), F32),
+            pltpu.VMEM((34, wide_rows, LANES), F32),
+            pltpu.VMEM((TURNED, wide_rows, rows), F32),
+            pltpu.VMEM((32, TILE, rows), F32),
+            pltpu.VMEM((TURNED + STRIP - 32, stack_rows, LANES), F32),
             pltpu.VMEM((AD_PLANES, stack_rows, LANES), F32),
-            pltpu.VMEM((16, rows, LANES), F32),
             pltpu.VMEM((32, rows, LANES), F32),
             pltpu.SemaphoreType.DMA((4,)),
         ],
         compiler_params=PARAMS,
-    )(spreading, *base, diffusion, *sides)
+    )(spreading, turned, side, north, water, metric_y, diffusion, from_west, from_east)
 
 
 def call_border(lat_info, spreading, diffusion, got_a, got_b, edge, advected, weights, outs):
@@ -542,6 +661,7 @@
     ring = [(i, (i + 1) % lon_count) for i in range(lon_count)]
     from_west = lax.ppermute(to_east, "lon", ring)
     from_east = lax.ppermute(to_west, "lon", [(j, i) for i, j in ring])
+    turned, side = call_flip(base)
     sides = (own, ownx, from_west, from_east)
     rows_a, rows_b, edge = call_edge(lat_info, base, sides)
 
@@ -555,10 +675,11 @@
             for a in range(1, lat_count - 1):
                 fixed.append((index(o, a), index(o, ((a + 1) ^ 1) - 1)))
             fixed.append((index(o, lat_count - 1), index((k - o) % lon_count, lat_count - 1)))
-        return lax.ppermute(x, ("lon", "lat"), fixed)
-
-    got_b = lax.switch(pivot, [functools.partial(across, k) for k in range(lon_count)], rows_b)
-    results = call_interior(spreading, base, diffusion, sides)
+        got = lax.ppermute(x, ("lon", "lat"), fixed)
+        return got, interior(spreading, turned, side, north, water, metric_y, diffusion, from_west, from_east)
+
+    interior = jax.jit(call_interior)
+    got_b, results = lax.switch(pivot, [functools.partial(across, k) for k in range(lon_count)], rows_b)
     return call_border(lat_info, spreading, diffusion, got_a, got_b, edge, results[4], results[5], results[:4])
 
 

time: 63 us -> 44.2 us (0.70)
  Pallas kernels: 39.7 us -> 24.5 us
  waiting for transfers between devices: 10.9 us -> 6.11 us
    pallas_call x1, Pallas kernels: 28.3 us -> 12.8 us  [call_interior(): pl.pallas_call(interior_kernel, out_shape=(shape(LEVELS, rows, cols),) *...]
    ppermute x1, waiting for transfers between devices: 4.93 us -> 0.01 us  [across(): got = lax.ppermute(x, ('lon', 'lat'), fixed)]
    pallas_call x0 -> x1, Pallas kernels: none -> 1.15 us  [call_flip(): pl.pallas_call(flip_kernel, out_shape=(shape(32, cols, rows), shape(2, co...]
    pallas_call x1, Pallas kernels: 4.07 us -> 3.43 us  [call_edge(): pl.pallas_call(edge_kernel, out_shape=(shape(PAIRS, TILE, LANES), shape(P...]
  transfers between devices with their start and end apart: 4 -> 4, of which waited for: 3 -> 2; matrix products, arithmetic and copies ran while one was open for 0% -> 0% of each run, Pallas kernels for 45% -> 32%
where the time goes in v3:
time: 44.2 us; the launch traced here: 43.6 us
  Pallas kernels  24.5 us (55%)
  starting transfers between devices  9.59 us (22%)
  waiting for transfers between devices  6.11 us (14%)
  local copies, waits for them, and re-layouts  1.67 us (4%)
  between operations  1.18 us (3%)
  loops' own time  0.49 us (1%)
    pallas_call x1, Pallas kernels, call_interior(): pl.pallas_call(interior_kernel, out_shape=(shape(LEVELS, rows, cols),) *...  12.8 us
    pallas_call x1, Pallas kernels, call_pack(): pl.pallas_call(pack_kernel, grid=(steps,), out_shape=(shape(2, rows, LANE...  4.82 us
    ppermute x1, starting transfers between devices, across(): got = lax.ppermute(x, ('lon', 'lat'), fixed)  4.49 us
    ppermute x1, waiting for transfers between devices, shards(): from_east = lax.ppermute(to_west, 'lon', [(j, i) for i, j in ring])  4.38 us
    ppermute x1, starting transfers between devices, shards(): from_west = lax.ppermute(to_east, 'lon', ring)  3.75 us
    pallas_call x1, Pallas kernels, call_edge(): pl.pallas_call(edge_kernel, out_shape=(shape(PAIRS, TILE, LANES), shape(P...  3.43 us
    pallas_call x1, Pallas kernels, call_border(): pl.pallas_call(border_kernel, grid=(1,), out_shape=(shape(LEVELS, rows, c...  2.29 us
    ppermute x1, waiting for transfers between devices, shards(): from_west = lax.ppermute(to_east, 'lon', ring)  1.72 us
  transfers between devices with their start and end apart: 4, of which 2 were waited for; matrix products, arithmetic and copies ran while one was open for 0% of the time, Pallas kernels for 32%

profile of v3, /device:TPU:103, one launch (start us, length us, event | category | flops | bytes accessed | tf_op | source)
XLA Modules:
  0.0 43.6 jit_solution(13494266465167937593)
XLA Ops:
  0.6 0.0 copy-start.7
  0.6 0.0 copy-start.6
  0.7 4.8 %shard_map.129 = (f32[2,128,128]{2,1,0:T(8,128)}, f32[3,8,128]{2,1,0:T(8,128)}, f32[160,128]{1,0:T(8,128)}, f32[160,128]{1,0:T(8,128)}) custom-call(f32[8,128,128]{2,1,0:T(8,128)} %t_ref.5, f32[8,128,128]{2,1,0:T(8,128)} %s_ref.5, f32[8,128,128]{2,1,0:T(8,128)} %u_ref.5, f32[8,128,128]{2,1,0:T(8,128)} %v_ref.5, s32[8,128,128]{2,1,0:T(8,128)} %w_ref.5, ...), custom_call_target="tpu_custom_call" | custom-call | tf_op jit(solution)/shard_map/pallas_call | solution.py:563
  5.5 3.8 %collective-permute-start.32 = (f32[160,128]{1,0:T(8,128)}, f32[160,128]{1,0:T(8,128)S(1)}, u32[]{:S(2)}, u32[]{:S(2)}) collective-permute-start(f32[160,128]{1,0:T(8,128)} %get-tuple-element.1174), channel_id=1, source_target_pairs={{0,8},{8,16},{16,24},{24,32},{32,40},{40,48},{48,56},{56,64},{64,7... | collective-permute-start | bytes 245768 | tf_op jit(solution)/shard_map/ppermute | solution.py:662
  9.3 0.0 collective-permute-start.33
  9.3 0.1 pad_add_fusion.lat_ref
  9.4 1.7 %collective-permute-done.32.fromw_ref = f32[160,128]{1,0:T(8,128)S(1)} collective-permute-done((f32[160,128]{1,0:T(8,128)}, f32[160,128]{1,0:T(8,128)S(1)}, u32[]{:S(2)}, u32[]{:S(2)}) %collective-permute-start.32) | collective-permute-done | bytes 81952 | tf_op jit(solution)/shard_map/ppermute | solution.py:662
  11.1 4.4 %collective-permute-done.33.frome_ref = f32[160,128]{1,0:T(8,128)S(1)} collective-permute-done((f32[160,128]{1,0:T(8,128)}, f32[160,128]{1,0:T(8,128)S(1)}, u32[]{:S(2)}, u32[]{:S(2)}) %collective-permute-start.33) | collective-permute-done | bytes 81952 | tf_op jit(solution)/shard_map/ppermute | solution.py:663
  15.5 0.0 copy-done.6
  15.5 0.0 copy-done.3
  15.5 0.0 copy-done.2
  15.5 0.0 copy-done.1
  15.5 0.0 copy-done
  15.5 0.0 copy-start.4
  15.5 0.9 %copy-done.4 = f32[2,128,128]{2,1,0:T(8,128)S(1)} copy-done((f32[2,128,128]{2,1,0:T(8,128)S(1)}, f32[2,128,128]{2,1,0:T(8,128)}, u32[]{:S(2)}) %copy-start.4) | copy-done | bytes 131096
  16.4 0.7 %copy-done.5 = f32[3,8,128]{2,1,0:T(8,128)S(1)} copy-done((f32[3,8,128]{2,1,0:T(8,128)S(1)}, f32[3,8,128]{2,1,0:T(8,128)}, u32[]{:S(2)}) %copy-start.5) | copy-done | bytes 12312
  17.1 3.4 %shard_map.130 = (f32[24,8,128]{2,1,0:T(8,128)S(1)}, f32[24,8,128]{2,1,0:T(8,128)S(1)}, f32[2,48,8,128]{3,2,1,0:T(8,128)S(1)}) custom-call(s32[2]{0:T(128)S(1)} %pad_add_fusion.lat_ref, f32[8,128,128]{2,1,0:T(8,128)S(1)} %copy-done, f32[8,128,128]{2,1,0:T(8,128)S(1)} %copy-done.1, f32[8,128,128]{2,1,0:T(8,128)S(1)} %copy-done.2, ...), custom_call_target="tpu_custom_call" | custom-call | tf_op jit(solution)/shard_map/pallas_call | solution.py:579
  20.6 0.0 copy-done.10
  20.6 1.3 %collective-permute-start.34 = (f32[24,8,128]{2,1,0:T(8,128)S(1)}, f32[24,8,128]{2,1,0:T(8,128)S(1)}, u32[]{:S(2)}, u32[]{:S(2)}) collective-permute-start(f32[24,8,128]{2,1,0:T(8,128)S(1)} %get-tuple-element.1176), channel_id=1, source_target_pairs={{0,1},{1,0},{2,3},{3,2},{4,5},{5,4},{6,7},{7,6},{8,9},{9,8},{10,11... | collective-permute-start | bytes 294920 | tf_op jit(solution)/shard_map/ppermute | solution.py:670
  22.1 0.0 copy-start.8
  22.1 0.0 copy-start.11
  22.1 1.2 %shard_map.131 = (f32[32,128,128]{2,1,0:T(8,128)S(1)}, f32[2,128,128]{2,1,0:T(8,128)S(1)}) custom-call(f32[8,128,128]{2,1,0:T(8,128)S(1)} %copy-done, f32[8,128,128]{2,1,0:T(8,128)S(1)} %copy-done.1, f32[8,128,128]{2,1,0:T(8,128)S(1)} %copy-done.2, f32[8,128,128]{2,1,0:T(8,128)S(1)} %copy-done.6, s32[8,128,128]{2,1,0:T(8,128)S(1)} %copy-done.7, ...), custom_call_target="tpu_custom_call" | custom-call | flops 8000000 | bytes 5000000 | tf_op jit(solution)/shard_map/pallas_call | solution.py:590
  23.3 0.0 copy-done.8
  23.3 0.0 copy-done.11
  23.3 0.0 copy-start.9
  23.3 17.8 %conditional.1 = (f32[24,8,128]{2,1,0:T(8,128)}, f32[8,128,128]{2,1,0:T(8,128)}, f32[8,128,128]{2,1,0:T(8,128)}, f32[8,128,128]{2,1,0:T(8,128)}, f32[8,128,128]{...) conditional(s32[]{:T(128)} %clamp.3, ...), branch_computations={%region_0.1_spmd, %region_1.2_spmd, %region_2.3_spmd, %region_3.4_... | conditional | bytes 393312 | solution.py:682
  23.4 4.5 %collective-permute-start.10 = (f32[24,8,128]{2,1,0:T(8,128)S(1)}, f32[24,8,128]{2,1,0:T(8,128)}, u32[]{:S(2)}, u32[]{:S(2)}) collective-permute-start(f32[24,8,128]{2,1,0:T(8,128)S(1)} %get-tuple-element.800), channel_id=1, source_target_pairs={{1,2},{2,1},{3,4},{4,3},{5,6},{6,5},{7,87},{9,10},{10,9},{11,12},{... | collective-permute-start | bytes 294920 | tf_op jit(solution)/shard_map/cond/branch_10_fun/ppermute | solution.py:678
  27.9 12.8 %call_interior.42 = (f32[8,128,128]{2,1,0:T(8,128)}, f32[8,128,128]{2,1,0:T(8,128)}, f32[8,128,128]{2,1,0:T(8,128)}, f32[8,128,128]{2,1,0:T(8,128)}, f32[36,32,1...) custom-call(f32[4,8]{1,0:T(4,128)S(1)} %get-tuple-element.801.coef_ref, f32[32,128,128]{2,1,0:T(8,128)S(1)} %get-tuple-element.802.turned_ref, ...), custom_call_target="tpu_custom_call" | custom-call | tf_op jit(solution)/shard_map/cond/branch_10_fun/jit(call_interior)/pallas_call | solution.py:604
  40.7 0.0 collective-permute-done.10
  41.1 0.0 collective-permute-done.34.a_ref
  41.2 0.0 copy-done.9
  41.2 2.3 %shard_map.132 = (f32[8,128,128]{2,1,0:T(8,128)}, f32[8,128,128]{2,1,0:T(8,128)}, f32[8,128,128]{2,1,0:T(8,128)}, f32[8,128,128]{2,1,0:T(8,128)}) custom-call(s32[2]{0:T(128)S(1)} %pad_add_fusion.lat_ref, f32[4,8]{1,0:T(4,128)S(1)} %copy-done.13, ...), custom_call_target="tpu_custom_call", output_to_operand_aliasing={{0}: (9, {}), {1}: (10, {}), {2}: (11, {}), {3}: (12, {})} | custom-call | tf_op jit(solution)/shard_map/pallas_call | solution.py:627
  (13 shorter events, 0.0 us)
Async XLA Ops:
  0.6 14.8 %copy-start.7 = (s32[8,128,128]{2,1,0:T(8,128)S(1)}, s32[8,128,128]{2,1,0:T(8,128)}, u32[]{:S(2)}) copy-start(s32[8,128,128]{2,1,0:T(8,128)} %w_ref.5) | copy-start | bytes 1572868
  0.6 14.8 %copy-start.6 = (f32[8,128,128]{2,1,0:T(8,128)S(1)}, f32[8,128,128]{2,1,0:T(8,128)}, u32[]{:S(2)}) copy-start(f32[8,128,128]{2,1,0:T(8,128)} %v_ref.5) | copy-start | bytes 1572868
  0.7 14.8 %copy-start.12 = (f32[128,128]{1,0:T(8,128)S(1)}, f32[128,128]{1,0:T(8,128)}, u32[]{:S(2)}) copy-start(f32[128,128]{1,0:T(8,128)} %my_ref.3) | copy-start | bytes 196612
  0.7 14.8 %copy-start.3 = (f32[128,128]{1,0:T(8,128)S(1)}, f32[128,128]{1,0:T(8,128)}, u32[]{:S(2)}) copy-start(f32[128,128]{1,0:T(8,128)} %mx_ref.5) | copy-start | bytes 196612
  0.7 14.8 %copy-start.2 = (f32[8,128,128]{2,1,0:T(8,128)S(1)}, f32[8,128,128]{2,1,0:T(8,128)}, u32[]{:S(2)}) copy-start(f32[8,128,128]{2,1,0:T(8,128)} %u_ref.5) | copy-start | bytes 1572868
  0.7 14.8 %copy-start.1 = (f32[8,128,128]{2,1,0:T(8,128)S(1)}, f32[8,128,128]{2,1,0:T(8,128)}, u32[]{:S(2)}) copy-start(f32[8,128,128]{2,1,0:T(8,128)} %s_ref.5) | copy-start | bytes 1572868
  0.7 14.8 %copy-start = (f32[8,128,128]{2,1,0:T(8,128)S(1)}, f32[8,128,128]{2,1,0:T(8,128)}, u32[]{:S(2)}) copy-start(f32[8,128,128]{2,1,0:T(8,128)} %t_ref.5) | copy-start | bytes 1572868
  5.5 16.4 %copy-start.14 = (s32[128]{0:T(128)S(1)}, s32[128]{0:T(128)}, u32[]{:S(2)}) copy-start(s32[128]{0:T(128)} %param.51) | copy-start | bytes 1540
  5.5 5.6 %collective-permute-start.32 = (f32[160,128]{1,0:T(8,128)}, f32[160,128]{1,0:T(8,128)S(1)}, u32[]{:S(2)}, u32[]{:S(2)}) collective-permute-start(f32[160,128]{1,0:T(8,128)} %get-tuple-element.1174), channel_id=1, source_target_pairs={{0,8},{8,16},{16,24},{24,32},{32,40},{40,48},{48,56},{56,64},{64,7... | collective-permute-start | bytes 245768 | tf_op jit(solution)/shard_map/ppermute | solution.py:662
  9.3 6.2 %collective-permute-start.33 = (f32[160,128]{1,0:T(8,128)}, f32[160,128]{1,0:T(8,128)S(1)}, u32[]{:S(2)}, u32[]{:S(2)}) collective-permute-start(f32[160,128]{1,0:T(8,128)} %get-tuple-element.1175), channel_id=1, source_target_pairs={{8,0},{16,8},{24,16},{32,24},{40,32},{48,40},{56,48},{64,56},{72,6... | collective-permute-start | bytes 245768 | tf_op jit(solution)/shard_map/ppermute | solution.py:663
  15.5 5.1 %copy-start.10 = (f32[160,128]{1,0:T(8,128)}, f32[160,128]{1,0:T(8,128)S(1)}, u32[]{:S(2)}) copy-start(f32[160,128]{1,0:T(8,128)S(1)} %collective-permute-done.33.frome_ref) | copy-start | bytes 245764
  15.5 0.9 %copy-start.4 = (f32[2,128,128]{2,1,0:T(8,128)S(1)}, f32[2,128,128]{2,1,0:T(8,128)}, u32[]{:S(2)}) copy-start(f32[2,128,128]{2,1,0:T(8,128)} %get-tuple-element.1172.own_ref) | copy-start | bytes 393220
  16.4 0.7 %copy-start.5 = (f32[3,8,128]{2,1,0:T(8,128)S(1)}, f32[3,8,128]{2,1,0:T(8,128)}, u32[]{:S(2)}) copy-start(f32[3,8,128]{2,1,0:T(8,128)} %get-tuple-element.1173.ownx_ref) | copy-start | bytes 36868
  20.6 2.7 %copy-start.13 = (f32[4,8]{1,0:T(4,128)S(1)}, f32[4,8]{1,0:T(4,128)}, u32[]{:S(2)}) copy-start(f32[4,8]{1,0:T(4,128)} %coef_ref.1) | copy-start | bytes 388
  20.6 20.6 %collective-permute-start.34 = (f32[24,8,128]{2,1,0:T(8,128)S(1)}, f32[24,8,128]{2,1,0:T(8,128)S(1)}, u32[]{:S(2)}, u32[]{:S(2)}) collective-permute-start(f32[24,8,128]{2,1,0:T(8,128)S(1)} %get-tuple-element.1176), channel_id=1, source_target_pairs={{0,1},{1,0},{2,3},{3,2},{4,5},{5,4},{6,7},{7,6},{8,9},{9,8},{10,11... | collective-permute-start | bytes 294920 | tf_op jit(solution)/shard_map/ppermute | solution.py:670
  22.1 1.2 %copy-start.8 = (f32[7,128,128]{2,1,0:T(8,128)S(1)}, f32[7,128,128]{2,1,0:T(8,128)}, u32[]{:S(2)}) copy-start(f32[7,128,128]{2,1,0:T(8,128)} %idf_hi.1) | copy-start | bytes 1376260
  22.1 1.2 %copy-start.11 = (f32[160,128]{1,0:T(8,128)S(1)}, f32[160,128]{1,0:T(8,128)}, u32[]{:S(2)}) copy-start(f32[160,128]{1,0:T(8,128)} %copy-done.10) | copy-start | bytes 245764
  23.3 17.9 %copy-start.9 = (f32[7,128,128]{2,1,0:T(8,128)S(1)}, f32[7,128,128]{2,1,0:T(8,128)}, u32[]{:S(2)}) copy-start(f32[7,128,128]{2,1,0:T(8,128)} %idf_hi.1) | copy-start | bytes 1376260
  23.4 17.4 %collective-permute-start.10 = (f32[24,8,128]{2,1,0:T(8,128)S(1)}, f32[24,8,128]{2,1,0:T(8,128)}, u32[]{:S(2)}, u32[]{:S(2)}) collective-permute-start(f32[24,8,128]{2,1,0:T(8,128)S(1)} %get-tuple-element.800), channel_id=1, source_target_pairs={{1,2},{2,1},{3,4},{4,3},{5,6},{6,5},{7,87},{9,10},{10,9},{11,12},{... | collective-permute-start | bytes 294920 | tf_op jit(solution)/shard_map/cond/branch_10_fun/ppermute | solution.py:678
